TPU v7x, 256 devices: a whole 4x4x8 slice. The times are simulated.
256 devices in a mesh: dp: 8 (over x, core), shard: 32 (over y, z).
Axes of the slice: x: 4, y: 4, z: 8, core: 2. Of those that a mesh axis runs over, the one named last changes fastest.
Arguments:
- queries: bfloat16 [2048, 256], P(('dp', 'shard')), may hold values from -1 to 1
- query_labels: int32 [2048], P(('dp', 'shard')), may hold values from 0 to 511, as said below
- positive_ids: int32 [2048, 64], P(('dp', 'shard')), may hold values from 0 to 32767, as said below
- positive_mask: int32 [2048, 64], P(('dp', 'shard')), may hold values from 0 to 1, as said below
- memory: bfloat16 [32768, 256], P('shard'), may hold values from -1 to 1
- memory_labels: int32 [32768], P('shard'), may hold values from 0 to 511
Outputs:
- precision: float32 [2048], P(('dp', 'shard'))
- query_grad: float32 [2048, 256], P(('dp', 'shard'))
Inputs may be any that keep to these rules, and one draw needn't show every extreme that they name: `positive_ids`: each query's used slots come first; they name distinct memory rows whose label equals the query's label, as many as min(64, rows of that class); unused slots hold 0. `positive_mask`: the first slot of every query is used. `query_labels`: every query's label is the label of some memory row.
All inputs are finite; a program needn't handle non-finite values.
Results may differ from a plain program's by a relative error of at most 0.0014.
Values may be sent and summed in bfloat16 or wider, within the bound.
A program may use at most 64 MiB of HBM per device.

v0:
```python
import jax
import jax.numpy as jnp
from jax import lax
from jax.sharding import PartitionSpec as P

TAU = 0.1
BLOCK = 8


def laid_out(tiles, dim):
    dims = list(tiles.shape[1:])
    dims[dim] *= tiles.shape[0]
    return jnp.moveaxis(tiles, 0, dim).reshape(dims)


def sent_to_all(array, axis):
    count = lax.axis_size(axis)
    return lax.all_to_all(
        jnp.broadcast_to(array[None], (count, *array.shape)), axis, 0, 0, tiled=True
    )


def gathered_copies(array, axis, dim):
    return laid_out(sent_to_all(array, axis), dim)


def side_by_side(arrays, axis, dim, along):
    columns = [a.reshape(*a.shape[:along], -1) for a in arrays]
    both = jnp.concatenate(columns, axis=along)
    out, at, finished = (lax.all_gather(both, axis, axis=dim, tiled=True), 0, [])
    for a, column in zip(arrays, columns):
        piece = out[..., at : at + column.shape[along]]
        finished.append(piece.reshape(*piece.shape[:along], *a.shape[along:]))
        at += column.shape[along]
    return tuple(finished)


def taken_together(array, axis):
    return sent_to_all(array, axis).sum(axis=0)


def in_one(arrays, axis):
    ends = [0]
    for a in arrays:
        ends.append(ends[-1] + a.size)
    running = taken_together(jnp.concatenate([a.ravel() for a in arrays]), axis)
    return tuple((running[b:e].reshape(a.shape) for a, b, e in zip(arrays, ends, ends[1:])))


def cut_along(array, dim, count):
    before, after = (array.shape[:dim], array.shape[dim + 1 :])
    return jnp.moveaxis(array.reshape(*before, count, -1, *after), dim, 0)


def summed_on_arrival(array, axis, dim):
    tiles = cut_along(array, dim, lax.axis_size(axis))
    arrived = lax.all_to_all(tiles, axis, split_axis=0, concat_axis=0, tiled=True)
    return arrived.sum(axis=0)


def positive_terms(positive, mask, rank_neg, slope_neg):
    maskf = mask.astype(jnp.float32)
    count = positive.shape[1]
    diff = (positive[:, None, :] - positive[:, :, None]) / TAU
    sig = jax.nn.sigmoid(diff)
    off = 1.0 - jnp.eye(count, dtype=jnp.float32)
    live = maskf[:, None, :] * off[None]
    rank_pos = 1.0 + jnp.sum(live * sig, axis=2)
    total = rank_pos + rank_neg
    found = jnp.sum(maskf, axis=1)
    precision = jnp.sum(maskf * rank_pos / total, axis=1) / found
    weight_neg = maskf * rank_pos / (found[:, None] * total * total)
    weight_pos = -maskf * rank_neg / (found[:, None] * total * total)
    slope = sig * (1.0 - sig) * off[None]
    spread = jnp.sum(maskf[:, None, :] * slope, axis=2)
    backed = jnp.sum(weight_pos[:, None, :] * slope, axis=2)
    dpos = (-weight_neg * slope_neg - weight_pos * spread + maskf * backed) / TAU
    return (precision, weight_neg, dpos)


def on_device(queries, query_labels, positive_ids, positive_mask, memory, memory_labels):
    owned = queries.shape[0]
    group_q = gathered_copies(queries, "shard", 0)
    ids, mask, labels = side_by_side((positive_ids, positive_mask, query_labels), "shard", 0, 1)
    local_rows = memory.shape[0]
    shard_index = lax.axis_index("shard")
    local_ids = ids - shard_index * local_rows
    inside = (local_ids >= 0) & (local_ids < local_rows)
    clipped = jnp.clip(local_ids, 0, local_rows - 1)
    scores = jnp.einsum("qd,rd->qr", group_q, memory, preferred_element_type=jnp.float32)
    row_iota = lax.broadcasted_iota(jnp.int32, (1, 1, local_rows), 2)
    partial_value = jnp.sum(
        jnp.where(local_ids[:, :, None] == row_iota, scores[:, None, :], 0.0), axis=2
    )
    positive = taken_together(partial_value, "shard")
    negative = memory_labels[None, :] != labels[:, None]
    count = positive.shape[1]
    blocks = count // BLOCK
    rows_q = scores.shape[0]

    def first_pass(step, carry):
        rank_part, slope_part = carry
        start = step * BLOCK
        column = lax.dynamic_slice_in_dim(positive, start, BLOCK, 1)
        sig = jax.nn.sigmoid((scores[:, None, :] - column[:, :, None]) / TAU)
        kept = jnp.where(negative[:, None, :], sig, 0.0)
        rank_part = lax.dynamic_update_slice_in_dim(rank_part, jnp.sum(kept, axis=2), start, 1)
        slope_part = lax.dynamic_update_slice_in_dim(
            slope_part, jnp.sum(kept * (1.0 - sig), axis=2), start, 1
        )
        return (rank_part, slope_part)

    empty = jnp.zeros((rows_q, count), jnp.float32)
    rank_part, slope_part = lax.fori_loop(0, blocks, first_pass, (empty, empty))
    rank_neg, slope_neg = in_one((rank_part, slope_part), "shard")
    precision, weight_neg, dpos = positive_terms(positive, mask, rank_neg, slope_neg)

    def second_pass(step, neg_acc):
        start = step * BLOCK
        column = lax.dynamic_slice_in_dim(positive, start, BLOCK, 1)
        weight = lax.dynamic_slice_in_dim(weight_neg, start, BLOCK, 1)
        sig = jax.nn.sigmoid((scores[:, None, :] - column[:, :, None]) / TAU)
        return neg_acc + jnp.sum(weight[:, :, None] * sig * (1.0 - sig), axis=1)

    zero_scores = jnp.zeros(scores.shape, jnp.float32)
    neg_acc = lax.fori_loop(0, blocks, second_pass, zero_scores)
    query_rows = jnp.arange(rows_q, dtype=jnp.int32)[:, None]
    pos_acc = zero_scores.at[query_rows, clipped].add(jnp.where(inside, dpos, 0.0))
    cotangent = jnp.where(negative, neg_acc / TAU, 0.0) + pos_acc
    mem_wide = memory.astype(jnp.float32)
    mine = summed_on_arrival(
        jnp.dot(
            cotangent, mem_wide, precision=lax.Precision.HIGHEST, preferred_element_type=jnp.float32
        ),
        "shard",
        0,
    )
    own_precision = lax.dynamic_slice_in_dim(precision, shard_index * owned, owned, 0)
    return (own_precision, mine)


def solution(mesh):
    return jax.shard_map(
        on_device,
        mesh=mesh,
        in_specs=(
            P(("dp", "shard"), None),
            P(("dp", "shard")),
            P(("dp", "shard"), None),
            P(("dp", "shard"), None),
            P("shard", None),
            P("shard"),
        ),
        out_specs=(P(("dp", "shard")), P(("dp", "shard"), None)),
        check_vma=False,
    )
```

profile of v0, /device:TPU:2, one launch (start us, length us, event | category | flops | bytes accessed | tf_op | source)
XLA Modules:
  0.0 471.9 jit_solution(8940306609593391410)
XLA Ops:
  0.6 1.4 broadcast_in_dim.103
  2.0 11.5 %all-to-all-start = ((bf16[32,8,256]{2,1,0:T(8,128)(2,1)}), bf16[32,8,256]{2,1,0:T(8,128)(2,1)S(1)}, u32[]{:S(2)}, u32[]{:S(2)}) async-start(bf16[32,8,256]{2,1,0:T(8,128)(2,1)} %broadcast_in_dim.103), calls=%async_computation | async-start | bytes 262144 | tf_op jit(solution)/shard_map/all_to_all | solution.py:18
  13.5 0.7 copy.29
  14.3 0.8 pad_add_fusion.1
  15.0 50.0 %all_gather.3 = s32[256,129]{1,0:T(8,128)S(1)} all-gather(s32[8,129]{1,0:T(8,128)S(1)} %pad_add_fusion.1), channel_id=1, replica_groups=mesh['dp'=8,'shard'=32] {'shard'}, dimensions={0}, use_global_device_ids=true | all-gather | bytes 136224 | tf_op jit(solution)/shard_map/all_gather | solution.py:30
  65.7 1.1 copy-done.1
  66.8 10.9 %select_reduce_fusion.1 = f32[256,64]{1,0:T(8,128)S(1)} fusion(f32[256,1024]{1,0:T(8,128)S(1)} %fusion.3, s32[256,64]{1,0:T(8,128)S(1)} %copy.32), kind=kLoop, calls=%fused_computation.12 | loop fusion | flops 50315264 | bytes 1179648 | tf_op jit(solution)/shard_map/reduce_sum | solution.py:92
  77.8 1.6 broadcast_in_dim.106
  79.4 7.0 %all-to-all-start.1 = ((f32[32,256,64]{1,2,0:T(8,128)}), f32[32,256,64]{1,2,0:T(8,128)S(1)}, u32[]{:S(2)}, u32[]{:S(2)}) async-start(f32[32,256,64]{1,2,0:T(8,128)} %broadcast_in_dim.106), calls=%async_computation.1 | async-start | bytes 4194304 | tf_op jit(solution)/shard_map/all_to_all | solution.py:18
  86.5 37.4 %all-to-all-done.1 = f32[32,256,64]{1,2,0:T(8,128)S(1)} async-done(((f32[32,256,64]{1,2,0:T(8,128)}), f32[32,256,64]{1,2,0:T(8,128)S(1)}, u32[]{:S(2)}, u32[]{:S(2)}) %all-to-all-start.1) | async-done | bytes 2097184 | tf_op jit(solution)/shard_map/all_to_all | solution.py:18
  124.1 62.3 %while.30 = (s32[]{:T(128)}, f32[256,64]{1,0:T(8,128)S(1)}, f32[256,64]{1,0:T(8,128)S(1)}, f32[256,1024]{1,0:T(8,128)}, f32[256,64]{1,0:T(8,128)S(1)}, /*index=5...) while((s32[]{:T(128)}, f32[256,64]{1,0:T(8,128)S(1)}, ...), condition=%wide.region_6.7_spmd.clone, body=%wide.region_3.0_spmd.clone.sunk | while | flops 21229572 | bytes 1651887 | solution.py:114
  124.5 5.7 %multiply_reduce_fusion.8 = (f32[256,8]{1,0:T(8,128)S(1)}, f32[256,8]{1,0:T(8,128)S(1)}) fusion(f32[256,8]{1,0:T(8,128)S(1)} %constant_dynamic-slice_fusion.6, f32[256,1024]{1,0:T(8,128)} %get-tuple-element.422, pred[256,1024]{1,0:T(8,128)(4,1)S(1)} %broadcast_compare_fusion.2), kind=kLoop, calls=%fused_computation.2.clone.1 | loop fusion | flops 20967424 | bytes 1335296 | tf_op jit(solution)/shard_map/while/body/eval_jaxpr/reduce_sum | solution.py:109
  130.2 0.6 dynamic_update_slice.18
  130.8 0.6 dynamic_update_slice.19
  131.8 5.7 %multiply_reduce_fusion.8 = (f32[256,8]{1,0:T(8,128)S(1)}, f32[256,8]{1,0:T(8,128)S(1)}) fusion(f32[256,8]{1,0:T(8,128)S(1)} %constant_dynamic-slice_fusion.6, f32[256,1024]{1,0:T(8,128)} %get-tuple-element.422, pred[256,1024]{1,0:T(8,128)(4,1)S(1)} %broadcast_compare_fusion.2), kind=kLoop, calls=%fused_computation.2.clone.1 | loop fusion | flops 20967424 | bytes 1335296 | tf_op jit(solution)/shard_map/while/body/eval_jaxpr/reduce_sum | solution.py:109
  137.5 0.9 dynamic_update_slice.18
  138.4 0.9 dynamic_update_slice.19
  139.7 5.7 %multiply_reduce_fusion.8 = (f32[256,8]{1,0:T(8,128)S(1)}, f32[256,8]{1,0:T(8,128)S(1)}) fusion(f32[256,8]{1,0:T(8,128)S(1)} %constant_dynamic-slice_fusion.6, f32[256,1024]{1,0:T(8,128)} %get-tuple-element.422, pred[256,1024]{1,0:T(8,128)(4,1)S(1)} %broadcast_compare_fusion.2), kind=kLoop, calls=%fused_computation.2.clone.1 | loop fusion | flops 20967424 | bytes 1335296 | tf_op jit(solution)/shard_map/while/body/eval_jaxpr/reduce_sum | solution.py:109
  145.4 0.9 dynamic_update_slice.18
  146.3 0.9 dynamic_update_slice.19
  147.5 5.7 %multiply_reduce_fusion.8 = (f32[256,8]{1,0:T(8,128)S(1)}, f32[256,8]{1,0:T(8,128)S(1)}) fusion(f32[256,8]{1,0:T(8,128)S(1)} %constant_dynamic-slice_fusion.6, f32[256,1024]{1,0:T(8,128)} %get-tuple-element.422, pred[256,1024]{1,0:T(8,128)(4,1)S(1)} %broadcast_compare_fusion.2), kind=kLoop, calls=%fused_computation.2.clone.1 | loop fusion | flops 20967424 | bytes 1335296 | tf_op jit(solution)/shard_map/while/body/eval_jaxpr/reduce_sum | solution.py:109
  153.2 0.9 dynamic_update_slice.18
  154.1 0.9 dynamic_update_slice.19
  155.4 5.7 %multiply_reduce_fusion.8 = (f32[256,8]{1,0:T(8,128)S(1)}, f32[256,8]{1,0:T(8,128)S(1)}) fusion(f32[256,8]{1,0:T(8,128)S(1)} %constant_dynamic-slice_fusion.6, f32[256,1024]{1,0:T(8,128)} %get-tuple-element.422, pred[256,1024]{1,0:T(8,128)(4,1)S(1)} %broadcast_compare_fusion.2), kind=kLoop, calls=%fused_computation.2.clone.1 | loop fusion | flops 20967424 | bytes 1335296 | tf_op jit(solution)/shard_map/while/body/eval_jaxpr/reduce_sum | solution.py:109
  161.1 0.9 dynamic_update_slice.18
  162.0 0.9 dynamic_update_slice.19
  163.2 5.7 %multiply_reduce_fusion.8 = (f32[256,8]{1,0:T(8,128)S(1)}, f32[256,8]{1,0:T(8,128)S(1)}) fusion(f32[256,8]{1,0:T(8,128)S(1)} %constant_dynamic-slice_fusion.6, f32[256,1024]{1,0:T(8,128)} %get-tuple-element.422, pred[256,1024]{1,0:T(8,128)(4,1)S(1)} %broadcast_compare_fusion.2), kind=kLoop, calls=%fused_computation.2.clone.1 | loop fusion | flops 20967424 | bytes 1335296 | tf_op jit(solution)/shard_map/while/body/eval_jaxpr/reduce_sum | solution.py:109
  168.9 0.9 dynamic_update_slice.18
  169.8 0.9 dynamic_update_slice.19
  171.1 5.7 %multiply_reduce_fusion.8 = (f32[256,8]{1,0:T(8,128)S(1)}, f32[256,8]{1,0:T(8,128)S(1)}) fusion(f32[256,8]{1,0:T(8,128)S(1)} %constant_dynamic-slice_fusion.6, f32[256,1024]{1,0:T(8,128)} %get-tuple-element.422, pred[256,1024]{1,0:T(8,128)(4,1)S(1)} %broadcast_compare_fusion.2), kind=kLoop, calls=%fused_computation.2.clone.1 | loop fusion | flops 20967424 | bytes 1335296 | tf_op jit(solution)/shard_map/while/body/eval_jaxpr/reduce_sum | solution.py:109
  176.8 0.9 dynamic_update_slice.18
  177.7 0.9 dynamic_update_slice.19
  178.9 5.7 %multiply_reduce_fusion.8 = (f32[256,8]{1,0:T(8,128)S(1)}, f32[256,8]{1,0:T(8,128)S(1)}) fusion(f32[256,8]{1,0:T(8,128)S(1)} %constant_dynamic-slice_fusion.6, f32[256,1024]{1,0:T(8,128)} %get-tuple-element.422, pred[256,1024]{1,0:T(8,128)(4,1)S(1)} %broadcast_compare_fusion.2), kind=kLoop, calls=%fused_computation.2.clone.1 | loop fusion | flops 20967424 | bytes 1335296 | tf_op jit(solution)/shard_map/while/body/eval_jaxpr/reduce_sum | solution.py:109
  184.6 0.9 dynamic_update_slice.18
  185.5 0.9 dynamic_update_slice.19
  186.6 5.7 %broadcast_in_dim.108 = f32[32,1,32768]{2,1,0:T(1,128)} broadcast(f32[32768]{0:T(1024)S(1)} %pad_maximum_fusion), dimensions={2} | broadcast | bytes 4325376 | tf_op jit(solution)/shard_map/broadcast_in_dim | solution.py:19
  192.3 7.2 %all-to-all-start.2 = ((f32[32,1,32768]{2,1,0:T(1,128)}), f32[32,1,32768]{2,1,0:T(1,128)}, u32[]{:S(2)}, u32[]{:S(2)}) async-start(f32[32,1,32768]{2,1,0:T(1,128)} %broadcast_in_dim.108), calls=%async_computation.2 | async-start | bytes 8388608 | tf_op jit(solution)/shard_map/all_to_all | solution.py:18
  200.1 2.4 multiply_reduce_fusion.3
  202.5 81.1 %all-to-all-done.2 = f32[32,1,32768]{2,1,0:T(1,128)} async-done(((f32[32,1,32768]{2,1,0:T(1,128)}), f32[32,1,32768]{2,1,0:T(1,128)}, u32[]{:S(2)}, u32[]{:S(2)}) %all-to-all-start.2) | async-done | bytes 4194336 | tf_op jit(solution)/shard_map/all_to_all | solution.py:18
  283.6 4.9 %reduce_sum.123 = f32[32768]{0:T(1024)S(1)} reduce(f32[32,1,32768]{2,1,0:T(1,128)} %all-to-all-done.2, f32[]{:T(128)} %constant.122.clone.1), dimensions={0,1}, to_apply=%region_7.8 | reduce | flops 1015808 | bytes 4325380 | tf_op jit(solution)/shard_map/reduce_sum | solution.py:39
  288.7 1.7 multiply_reduce_fusion.2
  290.7 50.5 %while.31 = (s32[]{:T(128)}, f32[256,1024]{1,0:T(8,128)S(1)}, f32[256,64]{0,1:T(8,128)S(1)}, f32[256,1024]{1,0:T(8,128)}, f32[256,64]{1,0:T(8,128)S(1)}, /*index=5*/s32[]{:T(128)}, s32[]{:T(128)}, s32[]{:T(128)}, s32[]{:T(128)}) while((s32[]{:T(128)}, f32[256,1024]{1,0:T(8,128)S(1)}, f32[256,64]{0,1:T(8,128)S(1)}, ...), condition=%wide.region_12.13_spmd.clone, body=%wide.region_10.12_spmd.clone.sunk | while | flops 19136516 | bytes 5308581 | solution.py:126
  290.9 5.7 %multiply_reduce_fusion.9 = f32[256,1024]{1,0:T(8,128)S(1)} fusion(f32[256,8]{1,0:T(8,128)S(1)} %constant_dynamic-slice_fusion.7, f32[256,1024]{1,0:T(8,128)} %get-tuple-element.451, f32[256,8]{1,0:T(8,128)S(1)} %copy.62), kind=kLoop, calls=%fused_computation.7.clone.1 | loop fusion | flops 18612224 | bytes 2113536 | tf_op jit(solution)/shard_map/while/body/eval_jaxpr/reduce_sum | solution.py:123
  296.6 0.4 select_add_fusion.2
  297.3 5.7 %multiply_reduce_fusion.9 = f32[256,1024]{1,0:T(8,128)S(1)} fusion(f32[256,8]{1,0:T(8,128)S(1)} %constant_dynamic-slice_fusion.7, f32[256,1024]{1,0:T(8,128)} %get-tuple-element.451, f32[256,8]{1,0:T(8,128)S(1)} %copy.62), kind=kLoop, calls=%fused_computation.7.clone.1 | loop fusion | flops 18612224 | bytes 2113536 | tf_op jit(solution)/shard_map/while/body/eval_jaxpr/reduce_sum | solution.py:123
  302.9 0.4 select_add_fusion.2
  303.6 5.7 %multiply_reduce_fusion.9 = f32[256,1024]{1,0:T(8,128)S(1)} fusion(f32[256,8]{1,0:T(8,128)S(1)} %constant_dynamic-slice_fusion.7, f32[256,1024]{1,0:T(8,128)} %get-tuple-element.451, f32[256,8]{1,0:T(8,128)S(1)} %copy.62), kind=kLoop, calls=%fused_computation.7.clone.1 | loop fusion | flops 18612224 | bytes 2113536 | tf_op jit(solution)/shard_map/while/body/eval_jaxpr/reduce_sum | solution.py:123
  309.2 0.4 select_add_fusion.2
  309.9 5.7 %multiply_reduce_fusion.9 = f32[256,1024]{1,0:T(8,128)S(1)} fusion(f32[256,8]{1,0:T(8,128)S(1)} %constant_dynamic-slice_fusion.7, f32[256,1024]{1,0:T(8,128)} %get-tuple-element.451, f32[256,8]{1,0:T(8,128)S(1)} %copy.62), kind=kLoop, calls=%fused_computation.7.clone.1 | loop fusion | flops 18612224 | bytes 2113536 | tf_op jit(solution)/shard_map/while/body/eval_jaxpr/reduce_sum | solution.py:123
  315.6 0.4 select_add_fusion.2
  316.2 5.7 %multiply_reduce_fusion.9 = f32[256,1024]{1,0:T(8,128)S(1)} fusion(f32[256,8]{1,0:T(8,128)S(1)} %constant_dynamic-slice_fusion.7, f32[256,1024]{1,0:T(8,128)} %get-tuple-element.451, f32[256,8]{1,0:T(8,128)S(1)} %copy.62), kind=kLoop, calls=%fused_computation.7.clone.1 | loop fusion | flops 18612224 | bytes 2113536 | tf_op jit(solution)/shard_map/while/body/eval_jaxpr/reduce_sum | solution.py:123
  321.9 0.4 select_add_fusion.2
  322.5 5.7 %multiply_reduce_fusion.9 = f32[256,1024]{1,0:T(8,128)S(1)} fusion(f32[256,8]{1,0:T(8,128)S(1)} %constant_dynamic-slice_fusion.7, f32[256,1024]{1,0:T(8,128)} %get-tuple-element.451, f32[256,8]{1,0:T(8,128)S(1)} %copy.62), kind=kLoop, calls=%fused_computation.7.clone.1 | loop fusion | flops 18612224 | bytes 2113536 | tf_op jit(solution)/shard_map/while/body/eval_jaxpr/reduce_sum | solution.py:123
  328.2 0.4 select_add_fusion.2
  328.8 5.7 %multiply_reduce_fusion.9 = f32[256,1024]{1,0:T(8,128)S(1)} fusion(f32[256,8]{1,0:T(8,128)S(1)} %constant_dynamic-slice_fusion.7, f32[256,1024]{1,0:T(8,128)} %get-tuple-element.451, f32[256,8]{1,0:T(8,128)S(1)} %copy.62), kind=kLoop, calls=%fused_computation.7.clone.1 | loop fusion | flops 18612224 | bytes 2113536 | tf_op jit(solution)/shard_map/while/body/eval_jaxpr/reduce_sum | solution.py:123
  334.5 0.4 select_add_fusion.2
  335.1 5.7 %multiply_reduce_fusion.9 = f32[256,1024]{1,0:T(8,128)S(1)} fusion(f32[256,8]{1,0:T(8,128)S(1)} %constant_dynamic-slice_fusion.7, f32[256,1024]{1,0:T(8,128)} %get-tuple-element.451, f32[256,8]{1,0:T(8,128)S(1)} %copy.62), kind=kLoop, calls=%fused_computation.7.clone.1 | loop fusion | flops 18612224 | bytes 2113536 | tf_op jit(solution)/shard_map/while/body/eval_jaxpr/reduce_sum | solution.py:123
  340.8 0.4 select_add_fusion.2
  341.8 113.2 %scatter_fusion = f32[262144]{0:T(1024)S(1)} fusion(f32[262144]{0:T(1024)S(1)} %bitcast.14, s32[16384]{0:T(1024)S(1)} %reshape.79, f32[16384]{0:T(1024)S(1)} %reshape.81), kind=kCustom, calls=%fused_computation | custom fusion | flops 16384 | bytes 262144
  455.1 1.3 convolution_bitcast_fusion
  456.4 4.0 all-to-all-start.3
  460.5 0.6 dynamic_slice.24
  461.1 10.2 %all-to-all-done.3 = f32[32,8,256]{2,1,0:T(8,128)S(1)} async-done(((f32[32,8,256]{2,1,0:T(8,128)}), f32[32,8,256]{2,1,0:T(8,128)S(1)}, u32[]{:S(2)}, u32[]{:S(2)}) %all-to-all-start.3) | async-done | bytes 262176 | tf_op jit(solution)/shard_map/all_to_all | solution.py:57
  471.3 0.6 reduce_sum.128
  (88 shorter events, 7.1 us)
Async XLA Ops:
  0.6 64.7 %copy-start = (bf16[1024,256]{1,0:T(8,128)(2,1)S(1)}, bf16[1024,256]{1,0:T(8,128)(2,1)}, u32[]{:S(2)}) copy-start(bf16[1024,256]{1,0:T(8,128)(2,1)} %param.14) | copy-start | bytes 1572868
  2.0 63.3 %all-to-all-start = ((bf16[32,8,256]{2,1,0:T(8,128)(2,1)}), bf16[32,8,256]{2,1,0:T(8,128)(2,1)S(1)}, u32[]{:S(2)}, u32[]{:S(2)}) async-start(bf16[32,8,256]{2,1,0:T(8,128)(2,1)} %broadcast_in_dim.103), calls=%async_computation | async-start | bytes 262144 | tf_op jit(solution)/shard_map/all_to_all | solution.py:18
  65.7 1.1 copy-start.1
  77.8 46.4 %copy-start.2 = (s32[1024]{0:T(1024)S(1)}, s32[1024]{0:T(1024)}, u32[]{:S(2)}) copy-start(s32[1024]{0:T(1024)} %param.15) | copy-start | bytes 12292
  79.4 44.5 %all-to-all-start.1 = ((f32[32,256,64]{1,2,0:T(8,128)}), f32[32,256,64]{1,2,0:T(8,128)S(1)}, u32[]{:S(2)}, u32[]{:S(2)}) async-start(f32[32,256,64]{1,2,0:T(8,128)} %broadcast_in_dim.106), calls=%async_computation.1 | async-start | bytes 4194304 | tf_op jit(solution)/shard_map/all_to_all | solution.py:18
  192.3 7.3 %copy-start.4 = (s32[2]{0:T(128)S(1)}, s32[2]{0:T(128)}, u32[]{:S(2)}) copy-start(s32[2]{0:T(128)} %constant.132) | copy-start | bytes 28
  192.3 7.4 %copy-start.3 = (s32[2]{0:T(128)S(1)}, s32[2]{0:T(128)}, u32[]{:S(2)}) copy-start(s32[2]{0:T(128)} %constant.135) | copy-start | bytes 28
  192.3 91.2 %all-to-all-start.2 = ((f32[32,1,32768]{2,1,0:T(1,128)}), f32[32,1,32768]{2,1,0:T(1,128)}, u32[]{:S(2)}, u32[]{:S(2)}) async-start(f32[32,1,32768]{2,1,0:T(1,128)} %broadcast_in_dim.108), calls=%async_computation.2 | async-start | bytes 8388608 | tf_op jit(solution)/shard_map/all_to_all | solution.py:18
  456.4 14.8 %all-to-all-start.3 = ((f32[32,8,256]{2,1,0:T(8,128)}), f32[32,8,256]{2,1,0:T(8,128)S(1)}, u32[]{:S(2)}, u32[]{:S(2)}) async-start(f32[32,8,256]{2,1,0:T(8,128)} %convolution_bitcast_fusion), calls=%async_computation.3 | async-start | bytes 524288 | tf_op jit(solution)/shard_map/all_to_all | solution.py:57
where the time goes:
time: 473 us; the launch traced here: 472 us
  other arithmetic  231 us (49%)
  waiting for transfers between devices  129 us (27%)
  blocking collectives  50 us (11%)
  starting transfers between devices  29.7 us (6%)
  local copies, waits for them, and re-layouts  29.1 us (6%)
    all_to_all x3, waiting for transfers between devices, sent_to_all(): lax.all_to_all(jnp.broadcast_to(array[None], (count, *array.shape)), axis...  118 us
    unnamed x6, other arithmetic  114 us
    all_gather x1, blocking collectives, side_by_side(): lax.all_gather(both, axis, axis=dim, tiled=True)  50 us
    reduce_sum x8, other arithmetic, first_pass(): jnp.sum(kept * (1.0 - sig), axis=2)  45.7 us
    reduce_sum x8, other arithmetic, second_pass(): return neg_acc + jnp.sum(weight[:, :, None] * sig * (1.0 - sig), axis=1)  45.4 us
    all_to_all x3, starting transfers between devices, sent_to_all(): lax.all_to_all(jnp.broadcast_to(array[None], (count, *array.shape)), axis...  25.7 us
    reduce_sum x1, other arithmetic, on_device(): jnp.sum(jnp.where(local_ids[:, :, None] == row_iota, scores[:, None, :],...  10.9 us
    all_to_all x1, waiting for transfers between devices, summed_on_arrival(): lax.all_to_all(tiles, axis, split_axis=0, concat_axis=0, tiled=True)  10.2 us
  transfers between devices with their start and end apart: 4, of which 3 were waited for; matrix products, arithmetic and copies ran while one was open for 1% of the time, Pallas kernels for 0%

commit v1 on v0

v1 whole, which is shorter than its diff:
```python
import functools

import jax
import jax.numpy as jnp
from jax import lax
from jax.experimental import pallas as pl
from jax.experimental.pallas import tpu as pltpu
from jax.sharding import PartitionSpec as P

F32 = jnp.float32
BF16 = jnp.bfloat16
I32 = jnp.int32
HALF_INV_TAU = 5.0
FAR = -1e6
MESH = pl.DeviceIdType.MESH
G = 8
KB = 4
JB = 16


def dot_nt(a, b):
    return lax.dot_general(a, b, (((1,), (1,)), ((), ())), preferred_element_type=F32)


def dot_nn(a, b):
    return lax.dot_general(a, b, (((1,), (0,)), ((), ())), preferred_element_type=F32)


def lane_gather(table, index):
    return jnp.take_along_axis(table, index, axis=1, mode="promise_in_bounds")


def kernel(
    n, q_ref, tab_ref, mem_ref, mlab_ref, prec_ref, grad_ref,
    qall, idall, s_ref, st_ref, inv_ref, ct_ref,
    ppart, prs, pown, pall, pt_ref, wq_ref, aux_ref,
    rsum, rpart, rrs, wdown, wdall, wdt_ref, gpart, grs,
    send_sem, recv_sem,
):
    me = lax.axis_index("shard")
    rows = mem_ref.shape[0]
    base = me * rows
    nb = rows // 128
    nh = n // 2
    my_half = me // nh

    def peer_of(d):
        return lax.rem(me + d, n)

    barrier = pltpu.get_barrier_semaphore()

    def greet(d, c):
        pl.semaphore_signal(barrier, inc=1, device_id={"shard": peer_of(d)}, device_id_type=MESH)
        return c

    lax.fori_loop(1, n, greet, 0)
    qall[me] = q_ref[...]
    idall[me] = tab_ref[...]
    pl.semaphore_wait(barrier, n - 1)

    def put(src, dst, phase, peer):
        pltpu.make_async_remote_copy(
            src_ref=src, dst_ref=dst, send_sem=send_sem.at[phase], recv_sem=recv_sem.at[phase],
            device_id={"shard": peer}, device_id_type=MESH,
        ).start()

    def await_blocks(sem, phase, buf, count):
        view = buf.at[pl.ds(0, count)]
        pltpu.make_async_copy(view, view, sem.at[phase]).wait()

    def spread_inputs(d, c):
        peer = peer_of(d)
        put(tab_ref, idall.at[me], 1, peer)
        put(q_ref, qall.at[me], 0, peer)
        return c

    lax.fori_loop(1, n, spread_inputs, 0)
    await_blocks(recv_sem, 1, idall, n - 1)
    await_blocks(recv_sem, 0, qall, n - 1)

    queries = qall[...].astype(F32).reshape(n * 8, q_ref.shape[1]).astype(BF16)
    mlab_t = jnp.transpose(jnp.concatenate([mlab_ref[...]] * 16, axis=0))
    id_t = [jnp.transpose(idall[pl.ds(h * nh, nh)].reshape(nh * 8, 128)) for h in range(2)]
    for a in range(nb):
        block = mem_ref[pl.ds(a * 128, 128), :]
        s_ref[:, pl.ds(a * 128, 128)] = dot_nt(queries, block)
        st = dot_nt(block, queries) * HALF_INV_TAU
        column = jnp.broadcast_to(mlab_t[:, a : a + 1], (128, 128))
        for h in range(2):
            label = id_t[h][64:65, :]
            st_ref[pl.ds(a * 128, 128), pl.ds(h * 128, 128)] = jnp.where(
                column != label, st[:, h * 128 : (h + 1) * 128], FAR
            )

    lane = lax.broadcasted_iota(I32, (8, 128), 1)

    def pick(b, c):
        local = idall[b] - base
        place = jnp.bitwise_and(local, 127)
        which = jnp.right_shift(local, 7)
        value = jnp.zeros((8, 128), F32)
        for a in range(nb):
            table = s_ref[pl.ds(pl.multiple_of(b * 8, 8), 8), pl.ds(a * 128, 128)]
            value = jnp.where(which == a, lane_gather(table, place), value)
        ppart[b] = jnp.where(lane < 64, value * HALF_INV_TAU, 0.0)
        return c

    lax.fori_loop(0, n, pick, 0)

    def send_positive(d, c):
        peer = peer_of(d)
        put(ppart.at[peer], prs.at[me], 2, peer)
        return c

    lax.fori_loop(1, n, send_positive, 0)
    prs[me] = ppart[me]
    await_blocks(recv_sem, 2, prs, n - 1)
    own = jnp.sum(prs[...], axis=0)
    pown[...] = own
    pall[me] = own

    def spread_positive(d, c):
        put(pown, pall.at[me], 3, peer_of(d))
        return c

    lax.fori_loop(1, n, spread_positive, 0)

    mask = jnp.where(jnp.logical_and(lane < 64, tab_ref[...] >= 0), 1.0, 0.0)
    own_t = jnp.transpose(jnp.concatenate([own] * 16, axis=0))
    mask_t = jnp.transpose(jnp.concatenate([mask] * 16, axis=0))
    off = jnp.where(
        lax.broadcasted_iota(I32, (64, 128), 0) == lax.broadcasted_iota(I32, (64, 128), 1), 0.0, 1.0
    )
    for i in range(8):
        col = jnp.broadcast_to(own_t[:64, i : i + 1], (64, 128))
        mcol = jnp.broadcast_to(mask_t[:64, i : i + 1], (64, 128)) * off
        t = jnp.tanh(col - own[i : i + 1, :])
        w = (1.0 - t * t) * (0.25 * off)
        wq_ref[i] = w
        aux_ref[i : i + 1, :] = 1.0 + jnp.sum(mcol * (0.5 + 0.5 * t), axis=0, keepdims=True)
        aux_ref[8 + i : 9 + i, :] = jnp.sum(mcol * w, axis=0, keepdims=True)

    def invert(b, c):
        local = idall[b] - base
        found = [jnp.full((8, 128), -1, I32) for _ in range(nb)]
        for k in range(64):
            here = jnp.broadcast_to(local[:, k : k + 1], (8, 128))
            for a in range(nb):
                found[a] = jnp.where(here == lane + a * 128, 64 + k, found[a])
        for a in range(nb):
            inv_ref[pl.ds(pl.multiple_of(b * 8, 8), 8), pl.ds(a * 128, 128)] = found[a]
        return c

    lax.fori_loop(0, n, invert, 0)

    await_blocks(recv_sem, 3, pall, n - 1)
    for h in range(2):
        pt_ref[h] = jnp.transpose(pall[pl.ds(h * nh, nh)].reshape(nh * 8, 128))[:64, :]

    def row_of(ref, k, h):
        return jnp.broadcast_to(ref[h, pl.ds(k, 1), :], (8, 128))

    def first_pass(h):
        def slots(kb, c):
            p = [row_of(pt_ref, kb * KB + i, h) for i in range(KB)]

            def step(g, acc):
                acc = list(acc)
                s = [
                    st_ref[pl.ds(pl.multiple_of(g * (8 * G), 8 * G) + 8 * v, 8), pl.ds(h * 128, 128)]
                    for v in range(G)
                ]
                for i in range(KB):
                    one = two = None
                    for v in range(G):
                        t = jnp.tanh(s[v] - p[i])
                        one = t if one is None else one + t
                        two = t * t if two is None else two + t * t
                    acc[2 * i] = acc[2 * i] + (one + float(G))
                    acc[2 * i + 1] = acc[2 * i + 1] + (float(G) - two)
                return tuple(acc)

            zero = jnp.zeros((8, 128), F32)
            acc = lax.fori_loop(0, rows // (8 * G), step, (zero,) * (2 * KB))
            for i in range(KB):
                rsum[pl.ds(kb * KB + i, 1), :] = 0.5 * jnp.sum(acc[2 * i], axis=0, keepdims=True)
                rsum[pl.ds(64 + kb * KB + i, 1), :] = 0.25 * jnp.sum(
                    acc[2 * i + 1], axis=0, keepdims=True
                )
            return c

        lax.fori_loop(0, 64 // KB, slots, 0)
        rpart[pl.ds(h * nh, nh)] = jnp.transpose(rsum[...]).reshape(nh, 8, 128)

        def send(d, c):
            owner = h * nh + lax.rem(me + d, nh)

            @pl.when(owner != me)
            def _():
                put(rpart.at[owner], rrs.at[me], 4 + h, owner)

            return c

        lax.fori_loop(0, nh, send, 0)

    def owner_terms(h):
        rrs[me] = rpart[me]
        await_blocks(recv_sem, 4 + h, rrs, n - 1)
        both = jnp.sum(rrs[...], axis=0)
        slope_neg = pltpu.roll(both, 64, axis=1)
        rank_neg = both
        rank_pos = aux_ref[0:8, :]
        spread = aux_ref[8:16, :]
        total = rank_pos + rank_neg
        found = jnp.sum(mask, axis=1, keepdims=True)
        share = mask / (found * total * total)
        weight_neg = share * rank_pos
        weight_pos = -share * rank_neg
        precision = jnp.sum(mask * rank_pos / total, axis=1, keepdims=True) / found
        prec_ref[...] = jnp.broadcast_to(precision, (8, 128))
        wp_t = jnp.transpose(jnp.concatenate([weight_pos] * 16, axis=0))
        for i in range(8):
            col = jnp.broadcast_to(wp_t[:64, i : i + 1], (64, 128))
            aux_ref[16 + i : 17 + i, :] = jnp.sum(col * wq_ref[i], axis=0, keepdims=True)
        backed = aux_ref[16:24, :]
        dpos = (mask * backed - weight_neg * slope_neg - weight_pos * spread) * (2.0 * HALF_INV_TAU)
        both = jnp.where(lane < 64, weight_neg * (0.5 * HALF_INV_TAU), pltpu.roll(dpos, 64, axis=1))
        wdown[...] = both
        wdall[me] = both

        def spread_weights(d, c):
            put(wdown, wdall.at[me], 6 + h, peer_of(d))
            return c

        lax.fori_loop(1, n, spread_weights, 0)

    def second_pass(h):
        @pl.when(my_half == h)
        def _():
            await_blocks(recv_sem, 6 + h, wdall, nh - 1)

        @pl.when(my_half != h)
        def _():
            await_blocks(recv_sem, 6 + h, wdall, nh)

        wdt_ref[h] = jnp.transpose(wdall[pl.ds(h * nh, nh)].reshape(nh * 8, 128))

        def block(jb, c):
            start = pl.multiple_of(jb * (8 * JB), 8 * JB)
            s = [st_ref[pl.ds(start + 8 * v, 8), pl.ds(h * 128, 128)] for v in range(JB)]

            def slot(k, acc):
                p = row_of(pt_ref, k, h)
                w = row_of(wdt_ref, k, h)
                out = []
                for v in range(JB):
                    t = jnp.tanh(s[v] - p)
                    out.append(acc[v] + w * (1.0 - t * t))
                return tuple(out)

            zero = jnp.zeros((8, 128), F32)
            acc = lax.fori_loop(0, 64, slot, (zero,) * JB, unroll=2)
            for v in range(JB):
                ct_ref[pl.ds(start + 8 * v, 8), :] = acc[v]
            return c

        lax.fori_loop(0, rows // (8 * JB), block, 0)
        hi, lo = [], []
        for a in range(nb):
            neg = jnp.transpose(ct_ref[pl.ds(a * 128, 128), :])
            pos = []
            for b in range(nh):
                index = inv_ref[pl.ds((h * nh + b) * 8, 8), pl.ds(a * 128, 128)]
                value = lane_gather(wdall[h * nh + b], jnp.bitwise_and(index, 127))
                pos.append(jnp.where(index >= 0, value, 0.0))
            cot = neg + jnp.concatenate(pos, axis=0)
            top = cot.astype(BF16)
            hi.append(top)
            lo.append((cot - top.astype(F32)).astype(BF16))
        memory = mem_ref[...]
        grad = dot_nn(jnp.concatenate(hi, axis=1), memory) + dot_nn(
            jnp.concatenate(lo, axis=1), memory
        )
        gpart[pl.ds(h * nh, nh)] = grad.reshape(nh, 8, grad.shape[1])

        def send(d, c):
            owner = h * nh + lax.rem(me + d, nh)

            @pl.when(owner != me)
            def _():
                put(gpart.at[owner], grs.at[me], 8 + h, owner)

            return c

        lax.fori_loop(0, nh, send, 0)

    first_pass(0)
    first_pass(1)
    for h in range(2):
        pl.when(my_half == h)(functools.partial(owner_terms, h))
    second_pass(0)
    second_pass(1)

    grs[me] = gpart[me]
    for h in range(2):
        @pl.when(my_half == h)
        def _():
            await_blocks(recv_sem, 8 + h, grs, n - 1)
            await_blocks(send_sem, 4 + h, rpart, nh - 1)
            await_blocks(send_sem, 5 - h, rpart, nh)
            await_blocks(send_sem, 8 + h, gpart, nh - 1)
            await_blocks(send_sem, 9 - h, gpart, nh)
            await_blocks(send_sem, 6 + h, wdall, n - 1)

    grad_ref[...] = jnp.sum(grs[...], axis=0)
    await_blocks(send_sem, 0, qall, n - 1)
    await_blocks(send_sem, 1, idall, n - 1)
    await_blocks(send_sem, 2, ppart, n - 1)
    await_blocks(send_sem, 3, pall, n - 1)


def on_device(n, queries, query_labels, positive_ids, positive_mask, memory, memory_labels):
    own, width = queries.shape
    rows = memory.shape[0]
    slots = positive_ids.shape[1]
    table = jnp.concatenate(
        [
            jnp.where(positive_mask > 0, positive_ids, -1),
            jnp.broadcast_to(query_labels[:, None], (own, slots)),
        ],
        axis=1,
    )
    vmem = pl.BlockSpec(memory_space=pltpu.VMEM)
    nq = n * own
    precision, grad = pl.pallas_call(
        functools.partial(kernel, n),
        out_shape=(
            jax.ShapeDtypeStruct((own, 128), F32),
            jax.ShapeDtypeStruct((own, width), F32),
        ),
        in_specs=[vmem] * 4,
        out_specs=(vmem, vmem),
        scratch_shapes=[
            pltpu.VMEM((n, own, width), BF16),
            pltpu.VMEM((n, own, 128), I32),
            pltpu.VMEM((nq, rows), F32),
            pltpu.VMEM((rows, nq), F32),
            pltpu.VMEM((nq, rows), I32),
            pltpu.VMEM((rows, 128), F32),
            pltpu.VMEM((n, own, 128), F32),
            pltpu.VMEM((n, own, 128), F32),
            pltpu.VMEM((own, 128), F32),
            pltpu.VMEM((n, own, 128), F32),
            pltpu.VMEM((2, slots, 128), F32),
            pltpu.VMEM((own, slots, 128), F32),
            pltpu.VMEM((24, 128), F32),
            pltpu.VMEM((128, 128), F32),
            pltpu.VMEM((n, own, 128), F32),
            pltpu.VMEM((n, own, 128), F32),
            pltpu.VMEM((own, 128), F32),
            pltpu.VMEM((n, own, 128), F32),
            pltpu.VMEM((2, 128, 128), F32),
            pltpu.VMEM((n, own, width), F32),
            pltpu.VMEM((n, own, width), F32),
            pltpu.SemaphoreType.DMA((10,)),
            pltpu.SemaphoreType.DMA((10,)),
        ],
        compiler_params=pltpu.CompilerParams(collective_id=0, has_side_effects=True),
    )(queries, table, memory, memory_labels.reshape(rows // 128, 128))
    return precision[:, 0], grad


def solution(mesh):
    n = mesh.shape["shard"]
    return jax.shard_map(
        functools.partial(on_device, n),
        mesh=mesh,
        in_specs=(
            P(("dp", "shard"), None),
            P(("dp", "shard")),
            P(("dp", "shard"), None),
            P(("dp", "shard"), None),
            P("shard", None),
            P("shard"),
        ),
        out_specs=(P(("dp", "shard")), P(("dp", "shard"), None)),
        check_vma=False,
    )
```

time: 473 us -> 95.8 us (0.20)
  the two profiles are of different devices: /device:TPU:2 before, /device:TPU:20 now
where the time goes in v1:
time: 95.8 us; the launch traced here: 95.5 us
  Pallas kernels  90.9 us (95%)
  local copies, waits for them, and re-layouts  2.64 us (3%)
  other arithmetic  1.36 us (1%)
    pallas_call x1, Pallas kernels, on_device(): pl.pallas_call(functools.partial(kernel, n), out_shape=(jax.ShapeDtypeStr...  90.9 us

profile of v1, /device:TPU:20, one launch (start us, length us, event | category | flops | bytes accessed | tf_op | source)
XLA Modules:
  0.0 95.5 jit_solution(318972544781506634)
XLA Ops:
  0.6 0.0 copy-start.1
  0.6 0.7 broadcast_in_dim.11
  1.4 0.0 copy-done.1
  1.4 0.7 compare_select_fusion
  2.1 0.7 pad_add_fusion.tab_ref
  2.7 90.9 %shard_map.77 = (f32[8,128]{1,0:T(8,128)}, f32[8,256]{1,0:T(8,128)}) custom-call(bf16[8,256]{1,0:T(8,128)(2,1)} %q_ref.1, s32[8,128]{1,0:T(8,128)} %pad_add_fusion.tab_ref, bf16[1024,256]{1,0:T(8,128)(2,1)} %mem_ref.1, s32[8,128]{1,0:T(8,128)} %bitcast.1), custom_call_target="tpu_custom_call" | custom-call | tf_op jit(solution)/shard_map/pallas_call | solution.py:335
  93.6 0.0 copy-start
  93.6 1.3 %slice_reduce_fusion = f32[8]{0:T(128)} fusion(f32[8,128]{1,0:T(8,128)} %get-tuple-element.4), kind=kLoop, calls=%fused_computation.1 | loop fusion | bytes 64 | tf_op jit(solution)/shard_map/slice | solution.py:370
  94.9 0.0 copy-done
  94.9 0.6 copy.9
Async XLA Ops:
  0.6 0.7 copy-start.1
  93.6 1.3 %copy-start = (f32[8,256]{1,0:T(8,128)S(1)}, f32[8,256]{1,0:T(8,128)}, u32[]{:S(2)}) copy-start(f32[8,256]{1,0:T(8,128)} %get-tuple-element.9) | copy-start | bytes 24580

commit v2 on v1

v2 whole, which is shorter than its diff:
```python
import functools

import jax
import jax.numpy as jnp
from jax import lax
from jax.experimental import pallas as pl
from jax.experimental.pallas import tpu as pltpu
from jax.sharding import PartitionSpec as P

F32 = jnp.float32
BF16 = jnp.bfloat16
I32 = jnp.int32
HALF_INV_TAU = 5.0
FAR = -1e6
MESH = pl.DeviceIdType.MESH
G = 8
KB = 4
JB = 8
NY, NZ = 4, 8
NC, NO = 4, 8
SPLIT = 12


def dot_nt(a, b):
    return lax.dot_general(a, b, (((1,), (1,)), ((), ())), preferred_element_type=F32)


def dot_nn(a, b):
    return lax.dot_general(a, b, (((1,), (0,)), ((), ())), preferred_element_type=F32)


def lane_gather(table, index):
    return jnp.take_along_axis(table, index, axis=1, mode="promise_in_bounds")


def owner_at(chunk, i):
    y, u = i // 2, i % 2
    return y * NZ + (chunk + 4 * u - 2 * y + 2 * NZ) % NZ


def twice(x):
    return jnp.transpose(jnp.concatenate([x, pltpu.roll(x, 96, axis=1)], axis=0))


def columns(x):
    return jnp.transpose(jnp.concatenate([x] * 16, axis=0))


def kernel(
    n, lab_ref, q_ref, id_ref, mask_ref, mlab_ref, mem_hbm, prec_ref, grad_ref,
    mem_ref, tab_ref, qall, tall, idall, s_ref, st_ref, inv_ref, ct_ref,
    ppart, prs, pown, pall, pt_ref, wq_ref, aux_ref,
    rsum, rpart, rrs, wdown, wdall, wt_ref, gpart, grs,
    send_sem, recv_sem, mem_sem,
):
    me = lax.axis_index("shard")
    rows = mem_ref.shape[0]
    base = me * rows
    nb = rows // 128
    my_y, my_z = me // NZ, me % NZ
    turn = my_z + 2 * my_y
    my_chunk = turn % NC
    my_place = my_chunk * NO + 2 * my_y + (turn % NZ) // NC

    def along_z(d):
        return my_y * NZ + (my_z + d) % NZ

    def along_y(d):
        return ((my_y + d) % NY) * NZ + my_z

    barrier = pltpu.get_barrier_semaphore()
    for peer in [along_z(d) for d in range(1, NZ)] + [along_y(d) for d in range(1, NY)]:
        pl.semaphore_signal(barrier, inc=1, device_id={"shard": peer}, device_id_type=MESH)

    load_memory = pltpu.make_async_copy(mem_hbm, mem_ref, mem_sem)
    load_memory.start()

    row = lax.broadcasted_iota(I32, (8, 64), 0)
    label = jnp.zeros((8, 64), I32)
    for i in range(8):
        label = jnp.where(row == i, lab_ref[i], label)
    tab_ref[:, 0:64] = jnp.where(mask_ref[...] > 0, id_ref[...], -1)
    tab_ref[:, 64:128] = label
    qall[me] = q_ref[...]
    tall[me] = tab_ref[...]

    def put(src, dst, send, recv, peer):
        pltpu.make_async_remote_copy(
            src_ref=src, dst_ref=dst, send_sem=send_sem.at[send], recv_sem=recv_sem.at[recv],
            device_id={"shard": peer}, device_id_type=MESH,
        ).start()

    def await_blocks(sem, index, buf, count):
        view = buf.at[pl.ds(0, count)]
        pltpu.make_async_copy(view, view, sem.at[index]).wait()

    pl.semaphore_wait(barrier, NZ + NY - 2)
    for d in (4, 3, 5, 2, 6, 1, 7):
        put(q_ref, qall.at[me], 0, 0, along_z(d))
        put(tab_ref, tall.at[me], 1, 1, along_z(d))
    line = pl.ds(my_y * NZ, NZ)
    await_blocks(recv_sem, 0, qall, NZ - 1)
    for d in (2, 1, 3):
        put(qall.at[line], qall.at[line], 0, 2, along_y(d))
    await_blocks(recv_sem, 1, tall, NZ - 1)
    for d in (2, 1, 3):
        put(tall.at[line], tall.at[line], 1, 3, along_y(d))
    load_memory.wait()
    await_blocks(recv_sem, 2, qall, n - NZ)
    await_blocks(recv_sem, 3, tall, n - NZ)

    lane = lax.broadcasted_iota(I32, (8, 128), 1)
    width = q_ref.shape[1]

    def queries_of(c):
        return jnp.concatenate([qall[owner_at(c, i)].astype(F32) for i in range(NO)], axis=0)

    def to_owners(c, src, dst, send, recv):
        def one(j, carry):
            i = (j + me) % NO
            owner = owner_at(c, i)

            @pl.when(owner != me)
            def _():
                put(src.at[c * NO + i], dst.at[me], send, recv + c, owner)

            return carry

        lax.fori_loop(0, NO, one, 0)

    def to_all(src, dst, send, recv):
        def one(d, carry):
            put(src, dst.at[my_place], send, recv + my_chunk, (me + d) % n)
            return carry

        lax.fori_loop(1, n, one, 0)

    def await_chunk(c, recv, buf):
        @pl.when(my_chunk == c)
        def _():
            await_blocks(recv_sem, recv + c, buf, NO - 1)

        @pl.when(my_chunk != c)
        def _():
            await_blocks(recv_sem, recv + c, buf, NO)

    for c in range(NC):
        s_ref[...] = dot_nt(queries_of(c).astype(BF16), mem_ref[...])
        for i in range(NO):
            table = tall[owner_at(c, i)]
            idall[c * NO + i] = table
            local = table - base
            place = jnp.bitwise_and(local, 127)
            which = jnp.right_shift(local, 7)
            value = jnp.zeros((8, 128), F32)
            for a in range(nb):
                block = s_ref[i * 8 : i * 8 + 8, a * 128 : a * 128 + 128]
                value = jnp.where(which == a, lane_gather(block, place), value)
            ppart[c * NO + i] = jnp.where(lane < 64, value * HALF_INV_TAU, 0.0)
        to_owners(c, ppart, prs, 2, 4)
    prs[me] = ppart[my_place]

    mlab_t = columns(mlab_ref[...])
    for c in range(NC):
        q = queries_of(c).astype(BF16)
        q = jnp.concatenate([q, q], axis=0)
        ids = idall[c * NO : c * NO + NO].reshape(NO * 8, 128)
        labels = jnp.transpose(jnp.concatenate([ids, ids], axis=0))[64:65, :]
        for a in range(nb):
            st = dot_nt(mem_ref[a * 128 : a * 128 + 128, :], q) * HALF_INV_TAU
            column = jnp.broadcast_to(mlab_t[:, a : a + 1], (128, 128))
            st_ref[c, a * 128 : a * 128 + 128, :] = jnp.where(column != labels, st, FAR)

    def invert(b, c):
        local = idall[b] - base
        found = [jnp.full((8, 128), -1, I32) for _ in range(nb)]
        for k in range(64):
            here = jnp.broadcast_to(local[:, k : k + 1], (8, 128))
            for a in range(nb):
                found[a] = jnp.where(here == lane + a * 128, 64 + k, found[a])
        for a in range(nb):
            inv_ref[b, :, a * 128 : a * 128 + 128] = found[a]
        return c

    lax.fori_loop(0, SPLIT, invert, 0)

    await_blocks(recv_sem, 4 + my_chunk, prs, n - 1)
    own = jnp.sum(prs[...], axis=0)
    pown[...] = own
    to_all(pown, pall, 3, 8)
    pall[my_place] = own

    mask = jnp.where(jnp.logical_and(lane < 64, tab_ref[...] >= 0), 1.0, 0.0)
    own_t = columns(own)
    mask_t = columns(mask)
    off = jnp.where(
        lax.broadcasted_iota(I32, (64, 128), 0) == lax.broadcasted_iota(I32, (64, 128), 1), 0.0, 1.0
    )
    for i in range(8):
        col = jnp.broadcast_to(own_t[:64, i : i + 1], (64, 128))
        mcol = jnp.broadcast_to(mask_t[:64, i : i + 1], (64, 128)) * off
        t = jnp.tanh(col - own[i : i + 1, :])
        w = (1.0 - t * t) * (0.25 * off)
        wq_ref[i] = w
        aux_ref[i : i + 1, :] = 1.0 + jnp.sum(mcol * (0.5 + 0.5 * t), axis=0, keepdims=True)
        aux_ref[8 + i : 9 + i, :] = jnp.sum(mcol * w, axis=0, keepdims=True)
    rsum[...] = jnp.zeros_like(rsum)

    lax.fori_loop(SPLIT, n, invert, 0)

    def first_pass(c, carry):
        await_chunk(c, 8, pall)
        pt_ref[c] = twice(pall[pl.ds(c * NO, NO)].reshape(NO * 8, 128))[:32, :]

        def slots(kb, carry):
            p = [
                jnp.broadcast_to(pt_ref[c, pl.ds(kb * KB + i, 1), :], (8, 128)) for i in range(KB)
            ]

            def step(g, acc):
                acc = list(acc)
                s = [
                    st_ref[c, pl.ds(pl.multiple_of(g * (8 * G), 8 * G) + 8 * v, 8), :]
                    for v in range(G)
                ]
                for i in range(KB):
                    one = two = None
                    for v in range(G):
                        t = jnp.tanh(s[v] - p[i])
                        one = t if one is None else one + t
                        two = t * t if two is None else two + t * t
                    acc[2 * i] = acc[2 * i] + (one + float(G))
                    acc[2 * i + 1] = acc[2 * i + 1] + (float(G) - two)
                return tuple(acc)

            zero = jnp.zeros((8, 128), F32)
            acc = lax.fori_loop(0, rows // (8 * G), step, (zero,) * (2 * KB), unroll=4)
            for i in range(KB):
                rsum[pl.ds(kb * KB + i, 1), :] = 0.5 * jnp.sum(acc[2 * i], axis=0, keepdims=True)
                rsum[pl.ds(64 + kb * KB + i, 1), :] = 0.25 * jnp.sum(
                    acc[2 * i + 1], axis=0, keepdims=True
                )
            return carry

        lax.fori_loop(0, 32 // KB, slots, 0)
        both = jnp.transpose(rsum[...])
        both = both[:64, :] + pltpu.roll(both[64:, :], 32, axis=1)
        rpart[pl.ds(c * NO, NO)] = both.reshape(NO, 8, 128)
        to_owners(c, rpart, rrs, 4, 12)
        return carry

    lax.fori_loop(0, NC, first_pass, 0)

    rrs[me] = rpart[my_place]
    await_blocks(recv_sem, 12 + my_chunk, rrs, n - 1)
    rank_neg = jnp.sum(rrs[...], axis=0)
    slope_neg = pltpu.roll(rank_neg, 64, axis=1)
    rank_pos = aux_ref[0:8, :]
    spread = aux_ref[8:16, :]
    total = rank_pos + rank_neg
    found = jnp.sum(mask, axis=1, keepdims=True)
    share = mask / (found * total * total)
    weight_neg = share * rank_pos
    weight_pos = -share * rank_neg
    wp_t = columns(weight_pos)
    for i in range(8):
        col = jnp.broadcast_to(wp_t[:64, i : i + 1], (64, 128))
        aux_ref[16 + i : 17 + i, :] = jnp.sum(col * wq_ref[i], axis=0, keepdims=True)
    backed = aux_ref[16:24, :]
    dpos = (mask * backed - weight_neg * slope_neg - weight_pos * spread) * (2.0 * HALF_INV_TAU)
    both = jnp.where(lane < 64, weight_neg * (0.5 * HALF_INV_TAU), pltpu.roll(dpos, 64, axis=1))
    wdown[...] = both
    to_all(wdown, wdall, 5, 16)
    wdall[my_place] = both
    precision = jnp.sum(mask * rank_pos / total, axis=1, keepdims=True) / found
    for i in range(8):
        prec_ref[i] = precision[i, 0]

    def second_pass(c, carry):
        await_chunk(c, 16, wdall)
        wt_ref[...] = twice(wdall[pl.ds(c * NO, NO)].reshape(NO * 8, 128))[:32, :]

        def block(jb, carry):
            start = pl.multiple_of(jb * (8 * JB), 8 * JB)
            s = [st_ref[c, pl.ds(start + 8 * v, 8), :] for v in range(JB)]

            def slot(k, acc):
                p = jnp.broadcast_to(pt_ref[c, pl.ds(k, 1), :], (8, 128))
                w = jnp.broadcast_to(wt_ref[pl.ds(k, 1), :], (8, 128))
                out = []
                for v in range(JB):
                    t = jnp.tanh(s[v] - p)
                    out.append(acc[v] + w * (1.0 - t * t))
                return tuple(out)

            zero = jnp.zeros((8, 128), F32)
            acc = lax.fori_loop(0, 32, slot, (zero,) * JB, unroll=16)
            for v in range(JB):
                ct_ref[pl.ds(start + 8 * v, 8), :] = acc[v]
            return carry

        lax.fori_loop(0, rows // (8 * JB), block, 0)
        hi, lo = [], []
        for a in range(nb):
            neg = jnp.transpose(ct_ref[a * 128 : a * 128 + 128, :])
            pos = []
            for i in range(NO):
                index = inv_ref[c * NO + i, :, a * 128 : a * 128 + 128]
                value = lane_gather(wdall[c * NO + i], jnp.bitwise_and(index, 127))
                pos.append(jnp.where(index >= 0, value, 0.0))
            cot = neg[:64, :] + neg[64:, :] + jnp.concatenate(pos, axis=0)
            top = cot.astype(BF16).astype(F32)
            hi.append(top)
            lo.append(cot - top)
        cot = jnp.concatenate([jnp.concatenate(hi, axis=1), jnp.concatenate(lo, axis=1)], axis=0)
        grad = dot_nn(cot.astype(BF16), mem_ref[...])
        gpart[pl.ds(c * NO, NO)] = (grad[:64, :] + grad[64:, :]).reshape(NO, 8, width)
        to_owners(c, gpart, grs, 6, 20)
        return carry

    lax.fori_loop(0, NC, second_pass, 0)

    grs[me] = gpart[my_place]
    await_blocks(recv_sem, 20 + my_chunk, grs, n - 1)
    grad_ref[...] = jnp.sum(grs[...], axis=0)
    for send, buf in enumerate((qall, tall, ppart, pall, rpart, wdall, gpart)):
        await_blocks(send_sem, send, buf, n - 1)


def on_device(n, queries, query_labels, positive_ids, positive_mask, memory, memory_labels):
    own, width = queries.shape
    rows = memory.shape[0]
    vmem = pl.BlockSpec(memory_space=pltpu.VMEM)
    smem = pl.BlockSpec(memory_space=pltpu.SMEM)
    return pl.pallas_call(
        functools.partial(kernel, n),
        out_shape=(
            jax.ShapeDtypeStruct((own,), F32),
            jax.ShapeDtypeStruct((own, width), F32),
        ),
        in_specs=[smem, vmem, vmem, vmem, vmem, pl.BlockSpec(memory_space=pl.ANY)],
        out_specs=(smem, vmem),
        scratch_shapes=[
            pltpu.VMEM((rows, width), BF16),
            pltpu.VMEM((own, 128), I32),
            pltpu.VMEM((n, own, width), BF16),
            pltpu.VMEM((n, own, 128), I32),
            pltpu.VMEM((n, own, 128), I32),
            pltpu.VMEM((NO * own, rows), F32),
            pltpu.VMEM((NC, rows, 128), F32),
            pltpu.VMEM((n, own, rows), I32),
            pltpu.VMEM((rows, 128), F32),
            pltpu.VMEM((n, own, 128), F32),
            pltpu.VMEM((n, own, 128), F32),
            pltpu.VMEM((own, 128), F32),
            pltpu.VMEM((n, own, 128), F32),
            pltpu.VMEM((NC, 32, 128), F32),
            pltpu.VMEM((own, 64, 128), F32),
            pltpu.VMEM((24, 128), F32),
            pltpu.VMEM((128, 128), F32),
            pltpu.VMEM((n, own, 128), F32),
            pltpu.VMEM((n, own, 128), F32),
            pltpu.VMEM((own, 128), F32),
            pltpu.VMEM((n, own, 128), F32),
            pltpu.VMEM((32, 128), F32),
            pltpu.VMEM((n, own, width), F32),
            pltpu.VMEM((n, own, width), F32),
            pltpu.SemaphoreType.DMA((7,)),
            pltpu.SemaphoreType.DMA((24,)),
            pltpu.SemaphoreType.DMA,
        ],
        compiler_params=pltpu.CompilerParams(collective_id=0, has_side_effects=True),
    )(
        query_labels, queries, positive_ids, positive_mask,
        memory_labels.reshape(rows // 128, 128), memory,
    )


def solution(mesh):
    n = mesh.shape["shard"]
    return jax.shard_map(
        functools.partial(on_device, n),
        mesh=mesh,
        in_specs=(
            P(("dp", "shard"), None),
            P(("dp", "shard")),
            P(("dp", "shard"), None),
            P(("dp", "shard"), None),
            P("shard", None),
            P("shard"),
        ),
        out_specs=(P(("dp", "shard")), P(("dp", "shard"), None)),
        check_vma=False,
    )
```

time: 95.8 us -> 80.9 us (0.84)
  the two profiles are of different devices: /device:TPU:20 before, /device:TPU:46 now
where the time goes in v2:
time: 80.9 us; the launch traced here: 80.7 us
  Pallas kernels  77.6 us (96%)
  local copies, waits for them, and re-layouts  2.47 us (3%)
    pallas_call x1, Pallas kernels, on_device(): pl.pallas_call(functools.partial(kernel, n), out_shape=(jax.ShapeDtypeStr...  77.6 us
    unnamed x4, local copies, waits for them, and re-layouts  2.47 us

profile of v2, /device:TPU:46, one launch (start us, length us, event | category | flops | bytes accessed | tf_op | source)
XLA Modules:
  0.0 80.7 jit_solution(5666208823895985110)
XLA Ops:
  0.6 77.6 %shard_map.77 = (f32[8]{0:T(128)}, f32[8,256]{1,0:T(8,128)}) custom-call(s32[8]{0:T(128)} %lab_ref.1, bf16[8,256]{1,0:T(8,128)(2,1)} %q_ref.1, s32[8,64]{1,0:T(8,128)} %id_ref.1, s32[8,64]{1,0:T(8,128)} %mask_ref.1, s32[8,128]{1,0:T(8,128)} %bitcast.1, bf16[1024,256]{1,0:T(8,128)(2,1)} %mem_hbm.1), custom_call_target="tpu_custom_call" | custom-call | tf_op jit(solution)/shard_map/pallas_call | solution.py:335
  78.3 0.0 copy-start
  78.3 0.7 copy-done
  78.9 0.5 copy.10
  79.4 1.3 %copy.11 = f32[8,256]{1,0:T(8,128)} copy(f32[8,256]{1,0:T(8,128)} %get-tuple-element.5) | data formatting | bytes 16384
Async XLA Ops:
  78.3 0.7 copy-start

commit v3 on v2

--- a/solution.py
+++ b/solution.py
@@ -13,11 +13,16 @@
 HALF_INV_TAU = 5.0
 FAR = -1e6
 MESH = pl.DeviceIdType.MESH
-G = 8
-KB = 4
+G = 16
+KB = 8
 JB = 8
+JC = 16
 NY, NZ = 4, 8
 NC, NO = 4, 8
+Z_IN, Z_TAB, Y_IN, Y_TAB, POS, POS_ALL, RANK, WEIGHT, GRAD, SPARE, N_RECV = (
+    0, 8, 16, 17, 18, 22, 26, 30, 34, 38, 41,
+)
+VMEM_LIMIT = 60 * 1024 * 1024
 SPLIT = 12
 
 
@@ -33,9 +38,14 @@
     return jnp.take_along_axis(table, index, axis=1, mode="promise_in_bounds")
 
 
+def static_owner_at(chunk, i):
+    y, u = i // 2, i % 2
+    return y * NZ + (chunk + 4 * u - 2 * y + 2 * NZ) % NZ
+
+
 def owner_at(chunk, i):
     y, u = i // 2, i % 2
-    return y * NZ + (chunk + 4 * u - 2 * y + 2 * NZ) % NZ
+    return y * NZ + lax.rem(chunk + (4 * u - 2 * y + 2 * NZ), NZ)
 
 
 def twice(x):
@@ -50,23 +60,25 @@
     n, lab_ref, q_ref, id_ref, mask_ref, mlab_ref, mem_hbm, prec_ref, grad_ref,
     mem_ref, tab_ref, qall, tall, idall, s_ref, st_ref, inv_ref, ct_ref,
     ppart, prs, pown, pall, pt_ref, wq_ref, aux_ref,
-    rsum, rpart, rrs, wdown, wdall, wt_ref, gpart, grs,
+    racc, squares, rpart, rrs, wdown, wdall, wt_ref, gpart, grs,
     send_sem, recv_sem, mem_sem,
 ):
     me = lax.axis_index("shard")
     rows = mem_ref.shape[0]
     base = me * rows
     nb = rows // 128
-    my_y, my_z = me // NZ, me % NZ
-    turn = my_z + 2 * my_y
-    my_chunk = turn % NC
-    my_place = my_chunk * NO + 2 * my_y + (turn % NZ) // NC
+    my_y, my_z = lax.div(me, NZ), lax.rem(me, NZ)
+    turn = lax.rem(my_z + 2 * my_y, NZ)
+    my_chunk = lax.rem(turn, NC)
+    my_place = my_chunk * NO + 2 * my_y + lax.div(turn, NC)
+    y_of = [lax.rem(my_y + d, NY) * NZ for d in range(NY)]
+    z_of = [lax.rem(my_z + d, NZ) for d in range(NZ)]
 
     def along_z(d):
-        return my_y * NZ + (my_z + d) % NZ
+        return y_of[0] + z_of[d]
 
     def along_y(d):
-        return ((my_y + d) % NY) * NZ + my_z
+        return y_of[d] + z_of[0]
 
     barrier = pltpu.get_barrier_semaphore()
     for peer in [along_z(d) for d in range(1, NZ)] + [along_y(d) for d in range(1, NY)]:
@@ -96,44 +108,43 @@
 
     pl.semaphore_wait(barrier, NZ + NY - 2)
     for d in (4, 3, 5, 2, 6, 1, 7):
-        put(q_ref, qall.at[me], 0, 0, along_z(d))
-        put(tab_ref, tall.at[me], 1, 1, along_z(d))
-    line = pl.ds(my_y * NZ, NZ)
-    await_blocks(recv_sem, 0, qall, NZ - 1)
+        put(q_ref, qall.at[me], 0, Z_IN + my_z, along_z(d))
+        put(tab_ref, tall.at[me], 1, Z_TAB + my_z, along_z(d))
     for d in (2, 1, 3):
-        put(qall.at[line], qall.at[line], 0, 2, along_y(d))
-    await_blocks(recv_sem, 1, tall, NZ - 1)
-    for d in (2, 1, 3):
-        put(tall.at[line], tall.at[line], 1, 3, along_y(d))
+        put(q_ref, qall.at[me], 0, Y_IN, along_y(d))
+        put(tab_ref, tall.at[me], 1, Y_TAB, along_y(d))
+    for d in (1, 7, 2, 6, 3, 5, 4):
+        slot = along_z(d)
+        pltpu.make_async_copy(qall.at[slot], qall.at[slot], recv_sem.at[Z_IN + z_of[d]]).wait()
+        for dy in (2, 1, 3):
+            put(qall.at[slot], qall.at[slot], 0, Y_IN, along_y(dy))
+        pltpu.make_async_copy(tall.at[slot], tall.at[slot], recv_sem.at[Z_TAB + z_of[d]]).wait()
+        for dy in (2, 1, 3):
+            put(tall.at[slot], tall.at[slot], 1, Y_TAB, along_y(dy))
     load_memory.wait()
-    await_blocks(recv_sem, 2, qall, n - NZ)
-    await_blocks(recv_sem, 3, tall, n - NZ)
+    await_blocks(recv_sem, Y_IN, qall, n - NZ)
+    await_blocks(recv_sem, Y_TAB, tall, n - NZ)
 
     lane = lax.broadcasted_iota(I32, (8, 128), 1)
     width = q_ref.shape[1]
 
     def queries_of(c):
-        return jnp.concatenate([qall[owner_at(c, i)].astype(F32) for i in range(NO)], axis=0)
-
-    def to_owners(c, src, dst, send, recv):
-        def one(j, carry):
-            i = (j + me) % NO
+        return jnp.concatenate([qall[static_owner_at(c, i)].astype(F32) for i in range(NO)], axis=0)
+
+    def to_owners(c, src, dst, send, recv, spare):
+        for i in range(NO):
             owner = owner_at(c, i)
-
-            @pl.when(owner != me)
-            def _():
-                put(src.at[c * NO + i], dst.at[me], send, recv + c, owner)
-
-            return carry
-
-        lax.fori_loop(0, NO, one, 0)
+            mine = owner == me
+            put(
+                src.at[c * NO + i], dst.at[jnp.where(mine, n, me)], send,
+                jnp.where(mine, spare, recv + c), jnp.where(mine, along_z(1), owner),
+            )
 
     def to_all(src, dst, send, recv):
-        def one(d, carry):
-            put(src, dst.at[my_place], send, recv + my_chunk, (me + d) % n)
-            return carry
-
-        lax.fori_loop(1, n, one, 0)
+        offsets = [(dy, dz) for dy in range(NY) for dz in range(NZ) if dy or dz]
+        offsets.sort(key=lambda o: -min(o[0], NY - o[0]) - min(o[1], NZ - o[1]))
+        for dy, dz in offsets:
+            put(src, dst.at[my_place], send, recv + my_chunk, y_of[dy] + z_of[dz])
 
     def await_chunk(c, recv, buf):
         @pl.when(my_chunk == c)
@@ -147,7 +158,7 @@
     for c in range(NC):
         s_ref[...] = dot_nt(queries_of(c).astype(BF16), mem_ref[...])
         for i in range(NO):
-            table = tall[owner_at(c, i)]
+            table = tall[static_owner_at(c, i)]
             idall[c * NO + i] = table
             local = table - base
             place = jnp.bitwise_and(local, 127)
@@ -157,7 +168,7 @@
                 block = s_ref[i * 8 : i * 8 + 8, a * 128 : a * 128 + 128]
                 value = jnp.where(which == a, lane_gather(block, place), value)
             ppart[c * NO + i] = jnp.where(lane < 64, value * HALF_INV_TAU, 0.0)
-        to_owners(c, ppart, prs, 2, 4)
+        to_owners(c, ppart, prs, 2, POS, SPARE)
     prs[me] = ppart[my_place]
 
     mlab_t = columns(mlab_ref[...])
@@ -184,10 +195,10 @@
 
     lax.fori_loop(0, SPLIT, invert, 0)
 
-    await_blocks(recv_sem, 4 + my_chunk, prs, n - 1)
-    own = jnp.sum(prs[...], axis=0)
+    await_blocks(recv_sem, POS + my_chunk, prs, n - 1)
+    own = jnp.sum(prs[0:n], axis=0)
     pown[...] = own
-    to_all(pown, pall, 3, 8)
+    to_all(pown, pall, 3, POS_ALL)
     pall[my_place] = own
 
     mask = jnp.where(jnp.logical_and(lane < 64, tab_ref[...] >= 0), 1.0, 0.0)
@@ -204,12 +215,13 @@
         wq_ref[i] = w
         aux_ref[i : i + 1, :] = 1.0 + jnp.sum(mcol * (0.5 + 0.5 * t), axis=0, keepdims=True)
         aux_ref[8 + i : 9 + i, :] = jnp.sum(mcol * w, axis=0, keepdims=True)
-    rsum[...] = jnp.zeros_like(rsum)
 
     lax.fori_loop(SPLIT, n, invert, 0)
 
-    def first_pass(c, carry):
-        await_chunk(c, 8, pall)
+    zero = jnp.zeros((8, 128), F32)
+
+    def first_pass(c, keep):
+        await_chunk(c, POS_ALL, pall)
         pt_ref[c] = twice(pall[pl.ds(c * NO, NO)].reshape(NO * 8, 128))[:32, :]
 
         def slots(kb, carry):
@@ -219,41 +231,49 @@
 
             def step(g, acc):
                 acc = list(acc)
-                s = [
-                    st_ref[c, pl.ds(pl.multiple_of(g * (8 * G), 8 * G) + 8 * v, 8), :]
-                    for v in range(G)
-                ]
+                at = [pl.ds(pl.multiple_of(g * (8 * G), 8 * G) + 8 * v, 8) for v in range(G)]
                 for i in range(KB):
                     one = two = None
                     for v in range(G):
-                        t = jnp.tanh(s[v] - p[i])
+                        t = jnp.tanh(st_ref[c, at[v], :] - p[i])
+                        tt = t * t
+                        if keep:
+                            squares[(c - 1) * 32 + kb * KB + i, at[v], :] = tt
                         one = t if one is None else one + t
-                        two = t * t if two is None else two + t * t
+                        two = tt if two is None else two + tt
                     acc[2 * i] = acc[2 * i] + (one + float(G))
                     acc[2 * i + 1] = acc[2 * i + 1] + (float(G) - two)
                 return tuple(acc)
 
-            zero = jnp.zeros((8, 128), F32)
             acc = lax.fori_loop(0, rows // (8 * G), step, (zero,) * (2 * KB), unroll=4)
             for i in range(KB):
-                rsum[pl.ds(kb * KB + i, 1), :] = 0.5 * jnp.sum(acc[2 * i], axis=0, keepdims=True)
-                rsum[pl.ds(64 + kb * KB + i, 1), :] = 0.25 * jnp.sum(
-                    acc[2 * i + 1], axis=0, keepdims=True
-                )
+                racc[kb * KB + i] = acc[2 * i]
+                racc[32 + kb * KB + i] = acc[2 * i + 1]
             return carry
 
         lax.fori_loop(0, 32 // KB, slots, 0)
-        both = jnp.transpose(rsum[...])
+        sums = jnp.sum(racc[...], axis=1)
+        gap = jnp.zeros((32, 128), F32)
+        both = jnp.transpose(
+            jnp.concatenate([0.5 * sums[:32, :], gap, 0.25 * sums[32:, :], gap], axis=0)
+        )
         both = both[:64, :] + pltpu.roll(both[64:, :], 32, axis=1)
         rpart[pl.ds(c * NO, NO)] = both.reshape(NO, 8, 128)
-        to_owners(c, rpart, rrs, 4, 12)
-        return carry
-
-    lax.fori_loop(0, NC, first_pass, 0)
+        to_owners(c, rpart, rrs, 4, RANK, SPARE + 1)
+
+    def with_squares(body):
+        def one(c, carry):
+            body(c, True)
+            return carry
+
+        lax.fori_loop(1, NC, one, 0)
+
+    first_pass(0, False)
+    with_squares(first_pass)
 
     rrs[me] = rpart[my_place]
-    await_blocks(recv_sem, 12 + my_chunk, rrs, n - 1)
-    rank_neg = jnp.sum(rrs[...], axis=0)
+    await_blocks(recv_sem, RANK + my_chunk, rrs, n - 1)
+    rank_neg = jnp.sum(rrs[0:n], axis=0)
     slope_neg = pltpu.roll(rank_neg, 64, axis=1)
     rank_pos = aux_ref[0:8, :]
     spread = aux_ref[8:16, :]
@@ -270,36 +290,37 @@
     dpos = (mask * backed - weight_neg * slope_neg - weight_pos * spread) * (2.0 * HALF_INV_TAU)
     both = jnp.where(lane < 64, weight_neg * (0.5 * HALF_INV_TAU), pltpu.roll(dpos, 64, axis=1))
     wdown[...] = both
-    to_all(wdown, wdall, 5, 16)
+    to_all(wdown, wdall, 5, WEIGHT)
     wdall[my_place] = both
     precision = jnp.sum(mask * rank_pos / total, axis=1, keepdims=True) / found
     for i in range(8):
         prec_ref[i] = precision[i, 0]
 
-    def second_pass(c, carry):
-        await_chunk(c, 16, wdall)
+    def second_pass(c, kept):
+        await_chunk(c, WEIGHT, wdall)
         wt_ref[...] = twice(wdall[pl.ds(c * NO, NO)].reshape(NO * 8, 128))[:32, :]
+        groups = JC if kept else JB
 
         def block(jb, carry):
-            start = pl.multiple_of(jb * (8 * JB), 8 * JB)
-            s = [st_ref[c, pl.ds(start + 8 * v, 8), :] for v in range(JB)]
-
-            def slot(k, acc):
-                p = jnp.broadcast_to(pt_ref[c, pl.ds(k, 1), :], (8, 128))
-                w = jnp.broadcast_to(wt_ref[pl.ds(k, 1), :], (8, 128))
-                out = []
-                for v in range(JB):
-                    t = jnp.tanh(s[v] - p)
-                    out.append(acc[v] + w * (1.0 - t * t))
-                return tuple(out)
-
-            zero = jnp.zeros((8, 128), F32)
-            acc = lax.fori_loop(0, 32, slot, (zero,) * JB, unroll=16)
-            for v in range(JB):
-                ct_ref[pl.ds(start + 8 * v, 8), :] = acc[v]
+            start = pl.multiple_of(jb * (8 * groups), 8 * groups)
+            at = [pl.ds(start + 8 * v, 8) for v in range(groups)]
+            acc = [zero] * groups
+            for k in range(32):
+                w = jnp.broadcast_to(wt_ref[k : k + 1, :], (8, 128))
+                if not kept:
+                    p = jnp.broadcast_to(pt_ref[c, k : k + 1, :], (8, 128))
+                for v in range(groups):
+                    if kept:
+                        tt = squares[(c - 1) * 32 + k, at[v], :]
+                    else:
+                        t = jnp.tanh(st_ref[c, at[v], :] - p)
+                        tt = t * t
+                    acc[v] = acc[v] + w * (1.0 - tt)
+            for v in range(groups):
+                ct_ref[at[v], :] = acc[v]
             return carry
 
-        lax.fori_loop(0, rows // (8 * JB), block, 0)
+        lax.fori_loop(0, rows // (8 * groups), block, 0)
         hi, lo = [], []
         for a in range(nb):
             neg = jnp.transpose(ct_ref[a * 128 : a * 128 + 128, :])
@@ -315,16 +336,18 @@
         cot = jnp.concatenate([jnp.concatenate(hi, axis=1), jnp.concatenate(lo, axis=1)], axis=0)
         grad = dot_nn(cot.astype(BF16), mem_ref[...])
         gpart[pl.ds(c * NO, NO)] = (grad[:64, :] + grad[64:, :]).reshape(NO, 8, width)
-        to_owners(c, gpart, grs, 6, 20)
-        return carry
-
-    lax.fori_loop(0, NC, second_pass, 0)
+        to_owners(c, gpart, grs, 6, GRAD, SPARE + 2)
+
+    second_pass(0, False)
+    with_squares(second_pass)
 
     grs[me] = gpart[my_place]
-    await_blocks(recv_sem, 20 + my_chunk, grs, n - 1)
-    grad_ref[...] = jnp.sum(grs[...], axis=0)
+    await_blocks(recv_sem, GRAD + my_chunk, grs, n - 1)
+    grad_ref[...] = jnp.sum(grs[0:n], axis=0)
+    for i, buf in enumerate((prs, rrs, grs)):
+        await_blocks(recv_sem, SPARE + i, buf, 1)
     for send, buf in enumerate((qall, tall, ppart, pall, rpart, wdall, gpart)):
-        await_blocks(send_sem, send, buf, n - 1)
+        await_blocks(send_sem, send, buf, n if send in (2, 4, 6) else n - 1)
 
 
 def on_device(n, queries, query_labels, positive_ids, positive_mask, memory, memory_labels):
@@ -338,7 +361,7 @@
             jax.ShapeDtypeStruct((own,), F32),
             jax.ShapeDtypeStruct((own, width), F32),
         ),
-        in_specs=[smem, vmem, vmem, vmem, vmem, pl.BlockSpec(memory_space=pl.ANY)],
+        in_specs=[smem, vmem, vmem, vmem, vmem, pl.BlockSpec(memory_space=pltpu.HBM)],
         out_specs=(smem, vmem),
         scratch_shapes=[
             pltpu.VMEM((rows, width), BF16),
@@ -351,25 +374,28 @@
             pltpu.VMEM((n, own, rows), I32),
             pltpu.VMEM((rows, 128), F32),
             pltpu.VMEM((n, own, 128), F32),
-            pltpu.VMEM((n, own, 128), F32),
+            pltpu.VMEM((n + 1, own, 128), F32),
             pltpu.VMEM((own, 128), F32),
             pltpu.VMEM((n, own, 128), F32),
             pltpu.VMEM((NC, 32, 128), F32),
             pltpu.VMEM((own, 64, 128), F32),
             pltpu.VMEM((24, 128), F32),
-            pltpu.VMEM((128, 128), F32),
+            pltpu.VMEM((64, 8, 128), F32),
+            pltpu.VMEM(((NC - 1) * 32, rows, 128), F32),
             pltpu.VMEM((n, own, 128), F32),
-            pltpu.VMEM((n, own, 128), F32),
+            pltpu.VMEM((n + 1, own, 128), F32),
             pltpu.VMEM((own, 128), F32),
             pltpu.VMEM((n, own, 128), F32),
             pltpu.VMEM((32, 128), F32),
             pltpu.VMEM((n, own, width), F32),
-            pltpu.VMEM((n, own, width), F32),
+            pltpu.VMEM((n + 1, own, width), F32),
             pltpu.SemaphoreType.DMA((7,)),
-            pltpu.SemaphoreType.DMA((24,)),
+            pltpu.SemaphoreType.DMA((N_RECV,)),
             pltpu.SemaphoreType.DMA,
         ],
-        compiler_params=pltpu.CompilerParams(collective_id=0, has_side_effects=True),
+        compiler_params=pltpu.CompilerParams(
+            collective_id=0, has_side_effects=True, vmem_limit_bytes=VMEM_LIMIT
+        ),
     )(
         query_labels, queries, positive_ids, positive_mask,
         memory_labels.reshape(rows // 128, 128), memory,

time: 80.9 us -> 71.8 us (0.89)
  the two profiles are of different devices: /device:TPU:46 before, /device:TPU:2 now
where the time goes in v3:
time: 71.8 us; the launch traced here: 70.8 us
  Pallas kernels  67.7 us (94%)
  local copies, waits for them, and re-layouts  2.47 us (3%)
    pallas_call x1, Pallas kernels, on_device(): pl.pallas_call(functools.partial(kernel, n), out_shape=(jax.ShapeDtypeStr...  67.7 us
    unnamed x4, local copies, waits for them, and re-layouts  2.47 us

profile of v3, /device:TPU:2, one launch (start us, length us, event | category | flops | bytes accessed | tf_op | source)
XLA Modules:
  0.0 70.8 jit_solution(9881348633443543880)
XLA Ops:
  0.6 67.7 %shard_map.77 = (f32[8]{0:T(128)}, f32[8,256]{1,0:T(8,128)}) custom-call(s32[8]{0:T(128)} %lab_ref.1, bf16[8,256]{1,0:T(8,128)(2,1)} %q_ref.1, s32[8,64]{1,0:T(8,128)} %id_ref.1, s32[8,64]{1,0:T(8,128)} %mask_ref.1, s32[8,128]{1,0:T(8,128)} %bitcast.1, bf16[1024,256]{1,0:T(8,128)(2,1)} %mem_hbm.1), custom_call_target="tpu_custom_call" | custom-call | tf_op jit(solution)/shard_map/pallas_call | solution.py:358
  68.3 0.0 copy-start
  68.3 0.7 copy-done
  69.0 0.5 copy.10
  69.5 1.3 %copy.11 = f32[8,256]{1,0:T(8,128)} copy(f32[8,256]{1,0:T(8,128)} %get-tuple-element.5) | data formatting | bytes 16384
Async XLA Ops:
  68.3 0.7 copy-start

commit v4 on v3

--- a/solution.py
+++ b/solution.py
@@ -10,20 +10,20 @@
 F32 = jnp.float32
 BF16 = jnp.bfloat16
 I32 = jnp.int32
+I16 = jnp.int16
 HALF_INV_TAU = 5.0
 FAR = -1e6
 MESH = pl.DeviceIdType.MESH
-G = 16
+G = 32
 KB = 8
 JB = 8
 JC = 16
 NY, NZ = 4, 8
 NC, NO = 4, 8
-Z_IN, Z_TAB, Y_IN, Y_TAB, POS, POS_ALL, RANK, WEIGHT, GRAD, SPARE, N_RECV = (
-    0, 8, 16, 17, 18, 22, 26, 30, 34, 38, 41,
+Z_IN, Z_TAB, Y_IN, Y_TAB, POS_Z, POS_Y, RANK, WEIGHT, GRAD, SPARE, N_RECV = (
+    0, 8, 16, 17, 18, 22, 26, 30, 34, 38, 40,
 )
 VMEM_LIMIT = 60 * 1024 * 1024
-SPLIT = 12
 
 
 def dot_nt(a, b):
@@ -58,8 +58,8 @@
 
 def kernel(
     n, lab_ref, q_ref, id_ref, mask_ref, mlab_ref, mem_hbm, prec_ref, grad_ref,
-    mem_ref, tab_ref, qall, tall, idall, s_ref, st_ref, inv_ref, ct_ref,
-    ppart, prs, pown, pall, pt_ref, wq_ref, aux_ref,
+    mem_ref, tab_ref, half_ref, qall, tall, idall, s_ref, st_ref, inv_ref, ct_ref,
+    ppart, pz, pys, py, pos_ref, pt_ref, wq_ref, aux_ref,
     racc, squares, rpart, rrs, wdown, wdall, wt_ref, gpart, grs,
     send_sem, recv_sem, mem_sem,
 ):
@@ -94,7 +94,8 @@
     tab_ref[:, 0:64] = jnp.where(mask_ref[...] > 0, id_ref[...], -1)
     tab_ref[:, 64:128] = label
     qall[me] = q_ref[...]
-    tall[me] = tab_ref[...]
+    half_ref[...] = tab_ref[...].astype(I16)
+    tall[me] = half_ref[...]
 
     def put(src, dst, send, recv, peer):
         pltpu.make_async_remote_copy(
@@ -109,10 +110,10 @@
     pl.semaphore_wait(barrier, NZ + NY - 2)
     for d in (4, 3, 5, 2, 6, 1, 7):
         put(q_ref, qall.at[me], 0, Z_IN + my_z, along_z(d))
-        put(tab_ref, tall.at[me], 1, Z_TAB + my_z, along_z(d))
+        put(half_ref, tall.at[me], 1, Z_TAB + my_z, along_z(d))
     for d in (2, 1, 3):
         put(q_ref, qall.at[me], 0, Y_IN, along_y(d))
-        put(tab_ref, tall.at[me], 1, Y_TAB, along_y(d))
+        put(half_ref, tall.at[me], 1, Y_TAB, along_y(d))
     for d in (1, 7, 2, 6, 3, 5, 4):
         slot = along_z(d)
         pltpu.make_async_copy(qall.at[slot], qall.at[slot], recv_sem.at[Z_IN + z_of[d]]).wait()
@@ -155,32 +156,7 @@
         def _():
             await_blocks(recv_sem, recv + c, buf, NO)
 
-    for c in range(NC):
-        s_ref[...] = dot_nt(queries_of(c).astype(BF16), mem_ref[...])
-        for i in range(NO):
-            table = tall[static_owner_at(c, i)]
-            idall[c * NO + i] = table
-            local = table - base
-            place = jnp.bitwise_and(local, 127)
-            which = jnp.right_shift(local, 7)
-            value = jnp.zeros((8, 128), F32)
-            for a in range(nb):
-                block = s_ref[i * 8 : i * 8 + 8, a * 128 : a * 128 + 128]
-                value = jnp.where(which == a, lane_gather(block, place), value)
-            ppart[c * NO + i] = jnp.where(lane < 64, value * HALF_INV_TAU, 0.0)
-        to_owners(c, ppart, prs, 2, POS, SPARE)
-    prs[me] = ppart[my_place]
-
     mlab_t = columns(mlab_ref[...])
-    for c in range(NC):
-        q = queries_of(c).astype(BF16)
-        q = jnp.concatenate([q, q], axis=0)
-        ids = idall[c * NO : c * NO + NO].reshape(NO * 8, 128)
-        labels = jnp.transpose(jnp.concatenate([ids, ids], axis=0))[64:65, :]
-        for a in range(nb):
-            st = dot_nt(mem_ref[a * 128 : a * 128 + 128, :], q) * HALF_INV_TAU
-            column = jnp.broadcast_to(mlab_t[:, a : a + 1], (128, 128))
-            st_ref[c, a * 128 : a * 128 + 128, :] = jnp.where(column != labels, st, FAR)
 
     def invert(b, c):
         local = idall[b] - base
@@ -193,36 +169,101 @@
             inv_ref[b, :, a * 128 : a * 128 + 128] = found[a]
         return c
 
-    lax.fori_loop(0, SPLIT, invert, 0)
-
-    await_blocks(recv_sem, POS + my_chunk, prs, n - 1)
-    own = jnp.sum(prs[0:n], axis=0)
-    pown[...] = own
-    to_all(pown, pall, 3, POS_ALL)
-    pall[my_place] = own
-
-    mask = jnp.where(jnp.logical_and(lane < 64, tab_ref[...] >= 0), 1.0, 0.0)
-    own_t = columns(own)
-    mask_t = columns(mask)
-    off = jnp.where(
-        lax.broadcasted_iota(I32, (64, 128), 0) == lax.broadcasted_iota(I32, (64, 128), 1), 0.0, 1.0
-    )
-    for i in range(8):
-        col = jnp.broadcast_to(own_t[:64, i : i + 1], (64, 128))
-        mcol = jnp.broadcast_to(mask_t[:64, i : i + 1], (64, 128)) * off
-        t = jnp.tanh(col - own[i : i + 1, :])
-        w = (1.0 - t * t) * (0.25 * off)
-        wq_ref[i] = w
-        aux_ref[i : i + 1, :] = 1.0 + jnp.sum(mcol * (0.5 + 0.5 * t), axis=0, keepdims=True)
-        aux_ref[8 + i : 9 + i, :] = jnp.sum(mcol * w, axis=0, keepdims=True)
-
-    lax.fori_loop(SPLIT, n, invert, 0)
+    for c in range(NC):
+        q = queries_of(c).astype(BF16)
+        s_ref[...] = dot_nt(q, mem_ref[...])
+        for i in range(NO):
+            table = tall[static_owner_at(c, i)].astype(I32)
+            idall[c * NO + i] = table
+            local = table - base
+            place = jnp.bitwise_and(local, 127)
+            which = jnp.right_shift(local, 7)
+            value = jnp.zeros((8, 128), F32)
+            for a in range(nb):
+                block = s_ref[i * 8 : i * 8 + 8, a * 128 : a * 128 + 128]
+                value = jnp.where(which == a, lane_gather(block, place), value)
+            value = jnp.where(lane < 64, value * HALF_INV_TAU, 0.0)
+            if i < NO // 2:
+                ppart[c, i] = value
+            else:
+                ppart[c, i - NO // 2] = ppart[c, i - NO // 2] + pltpu.roll(value, 64, axis=1)
+        for d in (4, 3, 5, 2, 6, 1, 7):
+            put(ppart.at[c], pz.at[c, my_z], 2, POS_Z + c, along_z(d))
+        pz[c, my_z] = ppart[c]
+
+        q = jnp.concatenate([q, q], axis=0)
+        ids = idall[c * NO : c * NO + NO].reshape(NO * 8, 128)
+        labels = jnp.transpose(jnp.concatenate([ids, ids], axis=0))[64:65, :]
+        for a in range(nb):
+            st = dot_nt(mem_ref[a * 128 : a * 128 + 128, :], q) * HALF_INV_TAU
+            column = jnp.broadcast_to(mlab_t[:, a : a + 1], (128, 128))
+            st_ref[c, a * 128 : a * 128 + 128, :] = jnp.where(column != labels, st, FAR)
+        lax.fori_loop(c * NO, c * NO + NO, invert, 0)
+
+    def positives_on(c):
+        await_blocks(recv_sem, POS_Z + c, pz.at[c], NZ - 1)
+        total = jnp.sum(pz[c], axis=0)
+        pys[c] = total
+        for d in (2, 1, 3):
+            put(pys.at[c], py.at[c, my_y], 3, POS_Y + c, along_y(d))
+        py[c, my_y] = total
+
+    positives_on(0)
+    positives_on(1)
+
+    def owner_terms():
+        my_i = my_place - my_chunk * NO
+        block = pos_ref[my_chunk, lax.rem(my_i, NO // 2)]
+        own = jnp.where(my_i >= NO // 2, pltpu.roll(block, 64, axis=1), block)
+        own = jnp.where(lane < 64, own, 0.0)
+        mask = jnp.where(jnp.logical_and(lane < 64, tab_ref[...] >= 0), 1.0, 0.0)
+        own_t = columns(own)
+        mask_t = columns(mask)
+        off = jnp.where(
+            lax.broadcasted_iota(I32, (64, 128), 0) == lax.broadcasted_iota(I32, (64, 128), 1), 0.0, 1.0
+        )
+        for i in range(8):
+            col = jnp.broadcast_to(own_t[:64, i : i + 1], (64, 128))
+            mcol = jnp.broadcast_to(mask_t[:64, i : i + 1], (64, 128)) * off
+            t = jnp.tanh(col - own[i : i + 1, :])
+            w = (1.0 - t * t) * (0.25 * off)
+            wq_ref[i] = w
+            aux_ref[i : i + 1, :] = 1.0 + jnp.sum(mcol * (0.5 + 0.5 * t), axis=0, keepdims=True)
+            aux_ref[8 + i : 9 + i, :] = jnp.sum(mcol * w, axis=0, keepdims=True)
+
+        rrs[me] = rpart[my_place]
+        await_blocks(recv_sem, RANK + my_chunk, rrs, n - 1)
+        rank_neg = jnp.sum(rrs[0:n], axis=0)
+        slope_neg = pltpu.roll(rank_neg, 64, axis=1)
+        rank_pos = aux_ref[0:8, :]
+        spread = aux_ref[8:16, :]
+        total = rank_pos + rank_neg
+        found = jnp.sum(mask, axis=1, keepdims=True)
+        share = mask / (found * total * total)
+        weight_neg = share * rank_pos
+        weight_pos = -share * rank_neg
+        wp_t = columns(weight_pos)
+        for i in range(8):
+            col = jnp.broadcast_to(wp_t[:64, i : i + 1], (64, 128))
+            aux_ref[16 + i : 17 + i, :] = jnp.sum(col * wq_ref[i], axis=0, keepdims=True)
+        backed = aux_ref[16:24, :]
+        dpos = (mask * backed - weight_neg * slope_neg - weight_pos * spread) * (2.0 * HALF_INV_TAU)
+        both = jnp.where(lane < 64, weight_neg * (0.5 * HALF_INV_TAU), pltpu.roll(dpos, 64, axis=1))
+        wdown[...] = both
+        to_all(wdown, wdall, 5, WEIGHT)
+        wdall[my_place] = both
+        precision = jnp.sum(mask * rank_pos / total, axis=1, keepdims=True) / found
+        for i in range(8):
+            prec_ref[i] = precision[i, 0]
 
     zero = jnp.zeros((8, 128), F32)
 
     def first_pass(c, keep):
-        await_chunk(c, POS_ALL, pall)
-        pt_ref[c] = twice(pall[pl.ds(c * NO, NO)].reshape(NO * 8, 128))[:32, :]
+        await_blocks(recv_sem, POS_Y + c, py.at[c], NY - 1)
+        both = jnp.sum(py[c], axis=0)
+        pos_ref[c] = both
+        both = both.reshape(NO * 4, 128)
+        pt_ref[c] = twice(jnp.concatenate([both, pltpu.roll(both, 64, axis=1)], axis=0))[:32, :]
 
         def slots(kb, carry):
             p = [
@@ -245,13 +286,22 @@
                     acc[2 * i + 1] = acc[2 * i + 1] + (float(G) - two)
                 return tuple(acc)
 
-            acc = lax.fori_loop(0, rows // (8 * G), step, (zero,) * (2 * KB), unroll=4)
+            acc = lax.fori_loop(0, rows // (8 * G), step, (zero,) * (2 * KB), unroll=2)
             for i in range(KB):
                 racc[kb * KB + i] = acc[2 * i]
                 racc[32 + kb * KB + i] = acc[2 * i + 1]
             return carry
 
-        lax.fori_loop(0, 32 // KB, slots, 0)
+        if keep:
+            lax.fori_loop(0, 16 // KB, slots, 0)
+
+            @pl.when(jnp.logical_and(c == NC - 1, my_chunk == 0))
+            def _():
+                owner_terms()
+
+            lax.fori_loop(16 // KB, 32 // KB, slots, 0)
+        else:
+            lax.fori_loop(0, 32 // KB, slots, 0)
         sums = jnp.sum(racc[...], axis=1)
         gap = jnp.zeros((32, 128), F32)
         both = jnp.transpose(
@@ -259,7 +309,7 @@
         )
         both = both[:64, :] + pltpu.roll(both[64:, :], 32, axis=1)
         rpart[pl.ds(c * NO, NO)] = both.reshape(NO, 8, 128)
-        to_owners(c, rpart, rrs, 4, RANK, SPARE + 1)
+        to_owners(c, rpart, rrs, 4, RANK, SPARE)
 
     def with_squares(body):
         def one(c, carry):
@@ -268,33 +318,20 @@
 
         lax.fori_loop(1, NC, one, 0)
 
+    def first_passes(c, keep):
+        first_pass(c, keep)
+
+        @pl.when(c == 1)
+        def _():
+            positives_on(3)
+
     first_pass(0, False)
-    with_squares(first_pass)
-
-    rrs[me] = rpart[my_place]
-    await_blocks(recv_sem, RANK + my_chunk, rrs, n - 1)
-    rank_neg = jnp.sum(rrs[0:n], axis=0)
-    slope_neg = pltpu.roll(rank_neg, 64, axis=1)
-    rank_pos = aux_ref[0:8, :]
-    spread = aux_ref[8:16, :]
-    total = rank_pos + rank_neg
-    found = jnp.sum(mask, axis=1, keepdims=True)
-    share = mask / (found * total * total)
-    weight_neg = share * rank_pos
-    weight_pos = -share * rank_neg
-    wp_t = columns(weight_pos)
-    for i in range(8):
-        col = jnp.broadcast_to(wp_t[:64, i : i + 1], (64, 128))
-        aux_ref[16 + i : 17 + i, :] = jnp.sum(col * wq_ref[i], axis=0, keepdims=True)
-    backed = aux_ref[16:24, :]
-    dpos = (mask * backed - weight_neg * slope_neg - weight_pos * spread) * (2.0 * HALF_INV_TAU)
-    both = jnp.where(lane < 64, weight_neg * (0.5 * HALF_INV_TAU), pltpu.roll(dpos, 64, axis=1))
-    wdown[...] = both
-    to_all(wdown, wdall, 5, WEIGHT)
-    wdall[my_place] = both
-    precision = jnp.sum(mask * rank_pos / total, axis=1, keepdims=True) / found
-    for i in range(8):
-        prec_ref[i] = precision[i, 0]
+    positives_on(2)
+    with_squares(first_passes)
+
+    @pl.when(my_chunk > 0)
+    def _():
+        owner_terms()
 
     def second_pass(c, kept):
         await_chunk(c, WEIGHT, wdall)
@@ -336,7 +373,7 @@
         cot = jnp.concatenate([jnp.concatenate(hi, axis=1), jnp.concatenate(lo, axis=1)], axis=0)
         grad = dot_nn(cot.astype(BF16), mem_ref[...])
         gpart[pl.ds(c * NO, NO)] = (grad[:64, :] + grad[64:, :]).reshape(NO, 8, width)
-        to_owners(c, gpart, grs, 6, GRAD, SPARE + 2)
+        to_owners(c, gpart, grs, 6, GRAD, SPARE + 1)
 
     second_pass(0, False)
     with_squares(second_pass)
@@ -344,10 +381,15 @@
     grs[me] = gpart[my_place]
     await_blocks(recv_sem, GRAD + my_chunk, grs, n - 1)
     grad_ref[...] = jnp.sum(grs[0:n], axis=0)
-    for i, buf in enumerate((prs, rrs, grs)):
+    for i, buf in enumerate((rrs, grs)):
         await_blocks(recv_sem, SPARE + i, buf, 1)
-    for send, buf in enumerate((qall, tall, ppart, pall, rpart, wdall, gpart)):
-        await_blocks(send_sem, send, buf, n if send in (2, 4, 6) else n - 1)
+    for send, buf, count in (
+        (0, qall, n - 1), (1, tall, n - 1), (4, rpart, n), (5, wdall, n - 1), (6, gpart, n),
+    ):
+        await_blocks(send_sem, send, buf, count)
+    for c in range(NC):
+        await_blocks(send_sem, 2, pz.at[c], NZ - 1)
+        await_blocks(send_sem, 3, py.at[c], NY - 1)
 
 
 def on_device(n, queries, query_labels, positive_ids, positive_mask, memory, memory_labels):
@@ -366,17 +408,19 @@
         scratch_shapes=[
             pltpu.VMEM((rows, width), BF16),
             pltpu.VMEM((own, 128), I32),
+            pltpu.VMEM((own, 128), I16),
             pltpu.VMEM((n, own, width), BF16),
-            pltpu.VMEM((n, own, 128), I32),
+            pltpu.VMEM((n, own, 128), I16),
             pltpu.VMEM((n, own, 128), I32),
             pltpu.VMEM((NO * own, rows), F32),
             pltpu.VMEM((NC, rows, 128), F32),
             pltpu.VMEM((n, own, rows), I32),
             pltpu.VMEM((rows, 128), F32),
-            pltpu.VMEM((n, own, 128), F32),
-            pltpu.VMEM((n + 1, own, 128), F32),
-            pltpu.VMEM((own, 128), F32),
-            pltpu.VMEM((n, own, 128), F32),
+            pltpu.VMEM((NC, NO // 2, own, 128), F32),
+            pltpu.VMEM((NC, NZ, NO // 2, own, 128), F32),
+            pltpu.VMEM((NC, NO // 2, own, 128), F32),
+            pltpu.VMEM((NC, NY, NO // 2, own, 128), F32),
+            pltpu.VMEM((NC, NO // 2, own, 128), F32),
             pltpu.VMEM((NC, 32, 128), F32),
             pltpu.VMEM((own, 64, 128), F32),
             pltpu.VMEM((24, 128), F32),

time: 71.8 us -> 74.2 us (1.033)
  Pallas kernels: 67.7 us -> 69.7 us
    pallas_call x1, Pallas kernels: 67.7 us -> 69.7 us  [on_device(): pl.pallas_call(functools.partial(kernel, n), out_shape=(jax.ShapeDtypeStr...]
where the time goes in v4:
time: 74.2 us; the launch traced here: 72.8 us
  Pallas kernels  69.7 us (94%)
  local copies, waits for them, and re-layouts  2.47 us (3%)
    pallas_call x1, Pallas kernels, on_device(): pl.pallas_call(functools.partial(kernel, n), out_shape=(jax.ShapeDtypeStr...  69.7 us
    unnamed x4, local copies, waits for them, and re-layouts  2.47 us

profile of v4, /device:TPU:2, one launch (start us, length us, event | category | flops | bytes accessed | tf_op | source)
XLA Modules:
  0.0 72.8 jit_solution(18408839835362773474)
XLA Ops:
  0.6 69.7 %shard_map.77 = (f32[8]{0:T(128)}, f32[8,256]{1,0:T(8,128)}) custom-call(s32[8]{0:T(128)} %lab_ref.1, bf16[8,256]{1,0:T(8,128)(2,1)} %q_ref.1, s32[8,64]{1,0:T(8,128)} %id_ref.1, s32[8,64]{1,0:T(8,128)} %mask_ref.1, s32[8,128]{1,0:T(8,128)} %bitcast.1, bf16[1024,256]{1,0:T(8,128)(2,1)} %mem_hbm.1), custom_call_target="tpu_custom_call" | custom-call | tf_op jit(solution)/shard_map/pallas_call | solution.py:400
  70.3 0.0 copy-start
  70.4 0.7 copy-done
  71.0 0.5 copy.10
  71.5 1.3 %copy.11 = f32[8,256]{1,0:T(8,128)} copy(f32[8,256]{1,0:T(8,128)} %get-tuple-element.5) | data formatting | bytes 16384
Async XLA Ops:
  70.3 0.7 copy-start

commit v5 on v0

v5 whole, which is shorter than its diff:
```python
import functools

import jax
import jax.numpy as jnp
from jax import lax
from jax.experimental import pallas as pl
from jax.experimental.pallas import tpu as pltpu
from jax.sharding import PartitionSpec as P

F32 = jnp.float32
BF16 = jnp.bfloat16
I32 = jnp.int32
I16 = jnp.int16
HALF_INV_TAU = 5.0
FAR = -1e6
MESH = pl.DeviceIdType.MESH
NY, NZ = 4, 8
NK, KB = 4, 8
G = 32
JC = 16
PIECES = 4
EARLY = (0, 2, 1)
VMEM_LIMIT = 60 * 1024 * 1024
DOWN, UP, RELAY, SIB, LAB, IN, TAB, POS, RANK, WEIGHT, GRAD, N_RECV = (
    0, 4, 8, 12, 15, 16, 17, 18, 19, 23, 27, 28,
)
S_MEM, S_LAB, S_IN, S_TAB, S_POS, S_RANK, S_WEIGHT, S_GRAD, N_SEND = range(9)


def dot_nt(a, b):
    return lax.dot_general(a, b, (((1,), (1,)), ((), ())), preferred_element_type=F32)


def dot_nn(a, b):
    return lax.dot_general(a, b, (((1,), (0,)), ((), ())), preferred_element_type=F32)


def lane_gather(table, index):
    return jnp.take_along_axis(table, index, axis=1, mode="promise_in_bounds")


def twice(x):
    return jnp.transpose(jnp.concatenate([x, pltpu.roll(x, 96, axis=1)], axis=0))


def columns(x):
    return jnp.transpose(jnp.concatenate([x] * 16, axis=0))


def kernel(
    lab_ref, q_ref, id_ref, mask_ref, mlab_ref, mem_hbm, prec_ref, grad_ref,
    mem_ref, labs, tab_ref, half_ref, qall, tall, idall, s_ref, st_ref, inv_ref, ct_ref,
    ppart, pz, pt_ref, wq_ref, aux_ref,
    racc, squares, rpart, rrs, ranks, wdown, wdall, wt_ref, gacc, gpart, grs,
    send_sem, recv_sem, mem_sem,
):
    dp = lax.axis_index("dp")
    me = lax.axis_index("shard")
    block_rows, width = mem_hbm.shape
    nb = block_rows // 128
    rows = NY * block_rows
    core = lax.rem(dp, 2)
    sibling = {"dp": dp + 1 - 2 * core, "shard": me}
    my_y, my_z = lax.div(me, NZ), lax.rem(me, NZ)
    y_at = [lax.rem(my_y + d, NY) for d in range(NY)]
    z_at = [lax.rem(my_z + d, NZ) for d in range(NZ)]
    along_z = [{"shard": my_y * NZ + z_at[d]} for d in range(NZ)]
    along_y = [{"shard": y_at[d] * NZ + my_z} for d in range(NY)]
    far_first = (4, 3, 5, 2, 6, 1, 7)

    barrier = pltpu.get_barrier_semaphore()
    for peer in [along_z[d] for d in far_first] + [along_y[d] for d in (2, 1, 3)] + [sibling]:
        pl.semaphore_signal(barrier, inc=1, device_id=peer, device_id_type=MESH)

    load_memory = pltpu.make_async_copy(mem_hbm, mem_ref.at[my_y], mem_sem)
    load_memory.start()

    row = lax.broadcasted_iota(I32, (8, 64), 0)
    label = jnp.zeros((8, 64), I32)
    for i in range(8):
        label = jnp.where(row == i, lab_ref[i], label)
    tab_ref[:, 0:64] = jnp.where(mask_ref[...] > 0, id_ref[...], -1)
    tab_ref[:, 64:128] = label
    half_ref[...] = tab_ref[...].astype(I16)
    qall[my_z] = q_ref[...]
    tall[my_z] = half_ref[...]
    labs[my_y] = mlab_ref[...]

    def put(src, dst, send, recv, peer):
        pltpu.make_async_remote_copy(
            src_ref=src, dst_ref=dst, send_sem=send_sem.at[send], recv_sem=recv_sem.at[recv],
            device_id=peer, device_id_type=MESH,
        ).start()

    def await_bytes(sem, index, view):
        pltpu.make_async_copy(view, view, sem.at[index]).wait()

    def await_line(recv, buf):
        await_bytes(recv_sem, recv, buf.at[pl.ds(0, NZ - 1)])

    def to_line(src, dst, send, recv):
        for d in far_first:
            put(src.at[z_at[d]], dst.at[my_z], send, recv, along_z[d])

    def on_line(src, dst, send, recv):
        for d in far_first:
            put(src, dst.at[my_z], send, recv, along_z[d])

    def part(piece):
        return pl.ds(pl.multiple_of(core * (block_rows // 2) + piece * 128, 128), 128)

    def hand_on(block, piece, recv):
        view = mem_ref.at[block, part(piece)]
        put(view, view, S_MEM, recv, sibling)

    pl.semaphore_wait(barrier, NZ + NY - 1)
    on_line(half_ref, tall, S_TAB, TAB)
    on_line(q_ref, qall, S_IN, IN)
    for up_piece, down_piece in ((0, 2), (1, 3), (2, 0), (3, 1)):
        for piece, recv, peer in ((up_piece, DOWN, along_y[1]), (down_piece, UP, along_y[3])):
            put(mem_hbm.at[part(piece)], mem_ref.at[my_y, part(piece)], S_MEM, recv + piece, peer)
    for d in (2, 1, 3):
        put(mlab_ref, labs.at[my_y], S_LAB, LAB, along_y[d])

    def landed(block, piece, recv):
        await_bytes(recv_sem, recv + piece, mem_ref.at[block, part(piece)])

    for step in range(2):
        piece = step
        landed(y_at[3], piece, DOWN)
        view = mem_ref.at[y_at[3], part(piece)]
        put(view, view, S_MEM, RELAY + piece, along_y[1])
        hand_on(y_at[3], piece, SIB)
        piece = step + 2
        landed(y_at[1], piece, UP)
        view = mem_ref.at[y_at[1], part(piece)]
        put(view, view, S_MEM, RELAY + piece, along_y[3])
        hand_on(y_at[1], piece, SIB + 1)

    await_line(TAB, tall)
    lane = lax.broadcasted_iota(I32, (8, 128), 1)
    for i in range(NZ):
        idall[i] = tall[i].astype(I32)

    def invert(b, y):
        local = idall[b] - (y * NZ + my_z) * block_rows
        found = [jnp.full((8, 128), -1, I32) for _ in range(nb)]
        for k in range(64):
            here = jnp.broadcast_to(local[:, k : k + 1], (8, 128))
            for a in range(nb):
                found[a] = jnp.where(here == lane + a * 128, 64 + k, found[a])
        for a in range(nb):
            inv_ref[b, y * nb + a] = found[a]
        return y

    def invert_owner(b):
        def one(y, c):
            invert(b, y)
            return c

        lax.fori_loop(0, NY, one, 0)

    owner = iter(range(NZ))
    for step in range(2):
        piece = step + 2
        landed(y_at[3], piece, DOWN)
        hand_on(y_at[3], piece, SIB)
        invert_owner(next(owner))
        piece = step
        landed(y_at[1], piece, UP)
        hand_on(y_at[1], piece, SIB + 1)
        invert_owner(next(owner))
    for piece in (0, 2, 1, 3):
        landed(y_at[2], piece, RELAY)
        hand_on(y_at[2], piece, SIB + 2)
        if piece in EARLY:
            invert_owner(next(owner))

    await_line(IN, qall)
    load_memory.wait()
    queries = jnp.concatenate([qall[i].astype(F32) for i in range(NZ)], axis=0).astype(BF16)
    for step, (d, arrived) in enumerate(((0, None), (3, SIB), (1, SIB + 1), (2, SIB + 2))):
        y = y_at[d]
        if arrived is not None:
            await_bytes(recv_sem, arrived, mem_ref.at[y, pl.ds(0, block_rows // 2)])
        s_ref[...] = dot_nt(queries, mem_ref[y])
        for i in range(NZ // 2):
            pair = None
            for j in (i, i + NZ // 2):
                local = idall[j] - (y * NZ + my_z) * block_rows
                place = jnp.bitwise_and(local, 127)
                which = jnp.right_shift(local, 7)
                value = jnp.zeros((8, 128), F32)
                for a in range(nb):
                    block = s_ref[j * 8 : j * 8 + 8, a * 128 : a * 128 + 128]
                    value = jnp.where(which == a, lane_gather(block, place), value)
                value = jnp.where(lane < 64, value * HALF_INV_TAU, 0.0)
                pair = value if pair is None else pair + pltpu.roll(value, 64, axis=1)
            ppart[i] = pair if step == 0 else ppart[i] + pair
    on_line(ppart, pz, S_POS, POS)
    pz[my_z] = ppart[...]

    for b in owner:
        invert_owner(b)
    await_bytes(recv_sem, LAB, labs.at[pl.ds(0, NY - 1)])
    queries = jnp.concatenate([queries, queries], axis=0)
    ids = idall[...].reshape(NZ * 8, 128)
    labels = jnp.transpose(jnp.concatenate([ids, ids], axis=0))[64:65, :]

    def score(y, c):
        lab_t = columns(labs[y])
        for a in range(nb):
            st = dot_nt(mem_ref[y, a * 128 : a * 128 + 128, :], queries) * HALF_INV_TAU
            column = jnp.broadcast_to(lab_t[:, a : a + 1], (128, 128))
            st_ref[pl.ds(pl.multiple_of(y * block_rows + a * 128, 128), 128), :] = jnp.where(
                column != labels, st, FAR
            )
        return c

    lax.fori_loop(0, NY, score, 0)

    await_line(POS, pz)
    pos = jnp.sum(pz[...], axis=0)
    half_line = NZ // 2
    own = jnp.where(lane < 64, pos[0], 0.0)
    for i in range(1, NZ):
        block = pos[i % half_line]
        block = pltpu.roll(block, 64, axis=1) if i >= half_line else block
        own = jnp.where(jnp.logical_and(my_z == i, lane < 64), block, own)
    pos = pos.reshape(half_line * 8, 128)
    pt_ref[...] = twice(jnp.concatenate([pos, pltpu.roll(pos, 64, axis=1)], axis=0))[:32, :]
    zero = jnp.zeros((8, 128), F32)
    mask = jnp.where(jnp.logical_and(lane < 64, tab_ref[...] >= 0), 1.0, 0.0)
    found = jnp.sum(mask, axis=1, keepdims=True)

    def first_pass(c):
        p = [jnp.broadcast_to(pt_ref[c * KB + i : c * KB + i + 1, :], (8, 128)) for i in range(KB)]

        def step(g, acc):
            acc = list(acc)
            at = [pl.ds(pl.multiple_of(g * (8 * G), 8 * G) + 8 * v, 8) for v in range(G)]
            for i in range(KB):
                one = two = None
                for v in range(G):
                    t = jnp.tanh(st_ref[at[v], :] - p[i])
                    tt = t * t
                    if c:
                        squares[(c - 1) * KB + i, at[v], :] = tt
                    one = t if one is None else one + t
                    two = tt if two is None else two + tt
                acc[2 * i] = acc[2 * i] + (one + float(G))
                acc[2 * i + 1] = acc[2 * i + 1] + (float(G) - two)
            return tuple(acc)

        acc = lax.fori_loop(0, rows // (8 * G), step, (zero,) * (2 * KB), unroll=2)
        for i in range(KB):
            racc[i] = acc[2 * i]
            racc[KB + i] = acc[2 * i + 1]
        sums = jnp.sum(racc[...], axis=1)
        spread = [jnp.zeros((8, 128), F32)] * 16
        spread[c] = 0.5 * sums[:KB, :]
        spread[8 + c] = 0.25 * sums[KB:, :]
        both = jnp.transpose(jnp.concatenate(spread, axis=0))
        both = both[:64, :] + pltpu.roll(both[64:, :], 32, axis=1)
        rpart[c] = both.reshape(NZ, 8, 128)
        to_line(rpart.at[c], rrs.at[c], S_RANK, RANK + c)
        rrs[c, my_z] = rpart[c, my_z]

    def positive_terms():
        own_t = columns(own)
        mask_t = columns(mask)
        off = jnp.where(
            lax.broadcasted_iota(I32, (64, 128), 0) == lax.broadcasted_iota(I32, (64, 128), 1),
            0.0, 1.0,
        )
        for i in range(8):
            col = jnp.broadcast_to(own_t[:64, i : i + 1], (64, 128))
            mcol = jnp.broadcast_to(mask_t[:64, i : i + 1], (64, 128)) * off
            t = jnp.tanh(col - own[i : i + 1, :])
            w = (1.0 - t * t) * (0.25 * off)
            wq_ref[i] = w
            aux_ref[i : i + 1, :] = 1.0 + jnp.sum(mcol * (0.5 + 0.5 * t), axis=0, keepdims=True)
            aux_ref[8 + i : 9 + i, :] = jnp.sum(mcol * w, axis=0, keepdims=True)

    def owner_terms(c):
        await_line(RANK + c, rrs.at[c])
        rank_neg = jnp.sum(rrs[c], axis=0)
        if c:
            rank_neg = rank_neg + ranks[...]
        ranks[...] = rank_neg
        rank_pos = aux_ref[0:8, :]
        total = rank_pos + rank_neg
        share = mask / (found * total * total)
        weight_neg = share * rank_pos
        both = jnp.where(lane < 64, weight_neg * (0.5 * HALF_INV_TAU), 0.0)
        if c == NK - 1:
            slope_neg = pltpu.roll(rank_neg, 64, axis=1)
            spread = aux_ref[8:16, :]
            weight_pos = -share * rank_neg
            wp_t = columns(weight_pos)
            for i in range(8):
                col = jnp.broadcast_to(wp_t[:64, i : i + 1], (64, 128))
                aux_ref[16 + i : 17 + i, :] = jnp.sum(col * wq_ref[i], axis=0, keepdims=True)
            backed = aux_ref[16:24, :]
            dpos = mask * backed - weight_neg * slope_neg - weight_pos * spread
            dpos = pltpu.roll(dpos * (2.0 * HALF_INV_TAU), 64, axis=1)
            both = jnp.where(lane < 64, both, dpos)
        wdown[c] = both
        on_line(wdown.at[c], wdall.at[c], S_WEIGHT, WEIGHT + c)
        wdall[c, my_z] = both
        if c == NK - 1:
            precision = jnp.sum(mask * rank_pos / total, axis=1, keepdims=True) / found
            for i in range(8):
                prec_ref[i] = precision[i, 0]

    def weigh(c, at, acc):
        for i in range(KB):
            w = jnp.broadcast_to(wt_ref[c * KB + i : c * KB + i + 1, :], (8, 128))
            if not c:
                p = jnp.broadcast_to(pt_ref[i : i + 1, :], (8, 128))
            for v in range(len(at)):
                if c:
                    tt = squares[(c - 1) * KB + i, at[v], :]
                else:
                    t = jnp.tanh(st_ref[at[v], :] - p)
                    tt = t * t
                acc[v] = acc[v] + w * (1.0 - tt)
        return acc

    def await_weights(c):
        await_line(WEIGHT + c, wdall.at[c])
        weights = twice(wdall[c].reshape(NZ * 8, 128))
        wt_ref[c * KB : c * KB + KB, :] = weights[c * KB : c * KB + KB, :]

    def second_pass(c):
        await_weights(c)

        def block(jb, carry):
            start = pl.multiple_of(jb * (8 * JC), 8 * JC)
            at = [pl.ds(start + 8 * v, 8) for v in range(JC)]
            acc = weigh(c, at, [ct_ref[at[v], :] if c else zero for v in range(JC)])
            for v in range(JC):
                ct_ref[at[v], :] = acc[v]
            return carry

        lax.fori_loop(0, rows // (8 * JC), block, 0, unroll=2)

    def last_pass(c):
        await_weights(c)
        gacc[...] = jnp.zeros_like(gacc)

        def block(a, carry):
            start = pl.multiple_of(a * 128, 128)
            at = [pl.ds(start + 8 * v, 8) for v in range(16)]
            acc = weigh(c, at, [ct_ref[at[v], :] for v in range(16)])
            neg = jnp.transpose(jnp.concatenate(acc, axis=0))
            pos = []
            for i in range(NZ):
                index = inv_ref[i, a]
                value = lane_gather(wdall[c, i], jnp.bitwise_and(index, 127))
                pos.append(jnp.where(index >= 0, value, 0.0))
            cot = neg[:64, :] + neg[64:, :] + jnp.concatenate(pos, axis=0)
            top = cot.astype(BF16).astype(F32)
            cot = jnp.concatenate([top, cot - top], axis=0).astype(BF16)
            memory = mem_ref[lax.div(a, nb), pl.ds(pl.multiple_of(lax.rem(a, nb) * 128, 128), 128), :]
            gacc[...] = gacc[...] + dot_nn(cot, memory)
            return carry

        lax.fori_loop(0, rows // 128, block, 0, unroll=2)
        grad = gacc[...]
        gpart[...] = (grad[:64, :] + grad[64:, :]).reshape(NZ, 8, width)
        to_line(gpart, grs, S_GRAD, GRAD)
        grs[my_z] = gpart[my_z]

    first_pass(0)
    first_pass(1)
    positive_terms()
    first_pass(2)
    owner_terms(0)
    first_pass(3)
    owner_terms(1)
    owner_terms(2)
    second_pass(0)
    owner_terms(3)
    second_pass(1)
    second_pass(2)
    last_pass(3)

    await_line(GRAD, grs)
    grad_ref[...] = jnp.sum(grs[...], axis=0)
    await_bytes(send_sem, S_MEM, mem_ref.at[pl.ds(0, 3)])
    await_bytes(send_sem, S_LAB, labs.at[pl.ds(0, NY - 1)])
    for send, buf in ((S_IN, qall), (S_TAB, tall), (S_POS, pz), (S_GRAD, grs)):
        await_bytes(send_sem, send, buf.at[pl.ds(0, NZ - 1)])
    for c in range(NK):
        await_bytes(send_sem, S_RANK, rrs.at[c, pl.ds(0, NZ - 1)])
        await_bytes(send_sem, S_WEIGHT, wdall.at[c, pl.ds(0, NZ - 1)])


def on_device(queries, query_labels, positive_ids, positive_mask, memory, memory_labels):
    own, width = queries.shape
    rows = memory.shape[0]
    vmem = pl.BlockSpec(memory_space=pltpu.VMEM)
    smem = pl.BlockSpec(memory_space=pltpu.SMEM)
    return pl.pallas_call(
        kernel,
        out_shape=(
            jax.ShapeDtypeStruct((own,), F32),
            jax.ShapeDtypeStruct((own, width), F32),
        ),
        in_specs=[smem, vmem, vmem, vmem, vmem, pl.BlockSpec(memory_space=pltpu.HBM)],
        out_specs=(smem, vmem),
        scratch_shapes=[
            pltpu.VMEM((NY, rows, width), BF16),
            pltpu.VMEM((NY, rows // 128, 128), I32),
            pltpu.VMEM((own, 128), I32),
            pltpu.VMEM((own, 128), I16),
            pltpu.VMEM((NZ, own, width), BF16),
            pltpu.VMEM((NZ, own, 128), I16),
            pltpu.VMEM((NZ, own, 128), I32),
            pltpu.VMEM((NZ * own, rows), F32),
            pltpu.VMEM((NY * rows, 128), F32),
            pltpu.VMEM((NZ, NY * rows // 128, own, 128), I32),
            pltpu.VMEM((NY * rows, 128), F32),
            pltpu.VMEM((NZ // 2, own, 128), F32),
            pltpu.VMEM((NZ, NZ // 2, own, 128), F32),
            pltpu.VMEM((32, 128), F32),
            pltpu.VMEM((own, 64, 128), F32),
            pltpu.VMEM((24, 128), F32),
            pltpu.VMEM((2 * KB, 8, 128), F32),
            pltpu.VMEM(((NK - 1) * KB, NY * rows, 128), F32),
            pltpu.VMEM((NK, NZ, own, 128), F32),
            pltpu.VMEM((NK, NZ, own, 128), F32),
            pltpu.VMEM((own, 128), F32),
            pltpu.VMEM((NK, own, 128), F32),
            pltpu.VMEM((NK, NZ, own, 128), F32),
            pltpu.VMEM((32, 128), F32),
            pltpu.VMEM((2 * NZ * own, width), F32),
            pltpu.VMEM((NZ, own, width), F32),
            pltpu.VMEM((NZ, own, width), F32),
            pltpu.SemaphoreType.DMA((N_SEND,)),
            pltpu.SemaphoreType.DMA((N_RECV,)),
            pltpu.SemaphoreType.DMA,
        ],
        compiler_params=pltpu.CompilerParams(
            collective_id=0, has_side_effects=True, vmem_limit_bytes=VMEM_LIMIT
        ),
    )(
        query_labels, queries, positive_ids, positive_mask,
        memory_labels.reshape(rows // 128, 128), memory,
    )


def solution(mesh):
    return jax.shard_map(
        on_device,
        mesh=mesh,
        in_specs=(
            P(("dp", "shard"), None),
            P(("dp", "shard")),
            P(("dp", "shard"), None),
            P(("dp", "shard"), None),
            P("shard", None),
            P("shard"),
        ),
        out_specs=(P(("dp", "shard")), P(("dp", "shard"), None)),
        check_vma=False,
    )
```

time: 473 us -> 69.1 us (0.15)
  other arithmetic: 231 us -> 0 us
  waiting for transfers between devices: 129 us -> 0 us
  Pallas kernels: 0 us -> 65.8 us
  blocking collectives: 50 us -> 0 us
  starting transfers between devices: 29.7 us -> 0 us
  local copies, waits for them, and re-layouts: 29.1 us -> 2.47 us
    all_to_all x4 -> x0, waiting for transfers between devices: 129 us -> none  [the longest x3 118 us: sent_to_all(): lax.all_to_all(jnp.broadcast_to(array[None], (count, *array.shape)), axis...]
    unnamed x6 -> x0, other arithmetic: 114 us -> none
    reduce_sum x23 -> x0, other arithmetic: 112 us -> none  [the longest x8 45.7 us: first_pass(): jnp.sum(kept * (1.0 - sig), axis=2)]
    pallas_call x0 -> x1, Pallas kernels: none -> 65.8 us  [on_device(): pl.pallas_call(kernel, out_shape=(jax.ShapeDtypeStruct((own,), F32), jax....]
    all_gather x1 -> x0, blocking collectives: 50 us -> none  [side_by_side(): lax.all_gather(both, axis, axis=dim, tiled=True)]
    all_to_all x4 -> x0, starting transfers between devices: 29.7 us -> none  [the longest x3 25.7 us: sent_to_all(): lax.all_to_all(jnp.broadcast_to(array[None], (count, *array.shape)), axis...]
    dynamic_update_slice x16 -> x0, local copies, waits for them, and re-layouts: 13.6 us -> none  [the longest x8 6.81 us: first_pass(): lax.dynamic_update_slice_in_dim(slope_part, jnp.sum(kept * (1.0 - sig), a...]
    broadcast_in_dim x6 -> x0, local copies, waits for them, and re-layouts: 8.75 us -> none  [the longest x3 8.72 us: sent_to_all(): jnp.broadcast_to(array[None], (count, *array.shape))]
  transfers between devices with their start and end apart: 4 -> 0, of which waited for: 3 -> 0; matrix products, arithmetic and copies ran while one was open for 1% -> 0% of each run, Pallas kernels for 0% -> 0%
where the time goes in v5:
time: 69.1 us; the launch traced here: 68.9 us
  Pallas kernels  65.8 us (95%)
  local copies, waits for them, and re-layouts  2.47 us (4%)
    pallas_call x1, Pallas kernels, on_device(): pl.pallas_call(kernel, out_shape=(jax.ShapeDtypeStruct((own,), F32), jax....  65.8 us
    unnamed x4, local copies, waits for them, and re-layouts  2.47 us

profile of v5, /device:TPU:2, one launch (start us, length us, event | category | flops | bytes accessed | tf_op | source)
XLA Modules:
  0.0 68.9 jit_solution(3894716633597938946)
XLA Ops:
  0.6 65.8 %shard_map.77 = (f32[8]{0:T(128)}, f32[8,256]{1,0:T(8,128)}) custom-call(s32[8]{0:T(128)} %lab_ref.1, bf16[8,256]{1,0:T(8,128)(2,1)} %q_ref.1, s32[8,64]{1,0:T(8,128)} %id_ref.1, s32[8,64]{1,0:T(8,128)} %mask_ref.1, s32[8,128]{1,0:T(8,128)} %bitcast.1, bf16[1024,256]{1,0:T(8,128)(2,1)} %mem_hbm.1), custom_call_target="tpu_custom_call" | custom-call | tf_op jit(solution)/shard_map/pallas_call | solution.py:405
  66.4 0.0 copy-start
  66.4 0.7 copy-done
  67.1 0.5 copy.10
  67.6 1.3 %copy.11 = f32[8,256]{1,0:T(8,128)} copy(f32[8,256]{1,0:T(8,128)} %get-tuple-element.5) | data formatting | bytes 16384
Async XLA Ops:
  66.4 0.7 copy-start

commit v6 on v5

--- a/solution.py
+++ b/solution.py
@@ -19,8 +19,8 @@
 G = 32
 JC = 16
 PIECES = 4
-EARLY = (0, 2, 1)
-VMEM_LIMIT = 60 * 1024 * 1024
+EARLY = ()
+VMEM_LIMIT = 67_043_328 - 327_680
 DOWN, UP, RELAY, SIB, LAB, IN, TAB, POS, RANK, WEIGHT, GRAD, N_RECV = (
     0, 4, 8, 12, 15, 16, 17, 18, 19, 23, 27, 28,
 )
@@ -51,7 +51,7 @@
     lab_ref, q_ref, id_ref, mask_ref, mlab_ref, mem_hbm, prec_ref, grad_ref,
     mem_ref, labs, tab_ref, half_ref, qall, tall, idall, s_ref, st_ref, inv_ref, ct_ref,
     ppart, pz, pt_ref, wq_ref, aux_ref,
-    racc, squares, rpart, rrs, ranks, wdown, wdall, wt_ref, gacc, gpart, grs,
+    racc, squares, rpart, rrs, ranks, wdown, wdall, wt_ref, memt_ref, cneg_ref, cpos_ref, gpart, grs,
     send_sem, recv_sem, mem_sem,
 ):
     dp = lax.axis_index("dp")
@@ -200,8 +200,8 @@
     on_line(ppart, pz, S_POS, POS)
     pz[my_z] = ppart[...]
 
-    for b in owner:
-        invert_owner(b)
+    for _ in range(2):
+        invert_owner(next(owner))
     await_bytes(recv_sem, LAB, labs.at[pl.ds(0, NY - 1)])
     queries = jnp.concatenate([queries, queries], axis=0)
     ids = idall[...].reshape(NZ * 8, 128)
@@ -215,6 +215,8 @@
             st_ref[pl.ds(pl.multiple_of(y * block_rows + a * 128, 128), 128), :] = jnp.where(
                 column != labels, st, FAR
             )
+            flipped = jnp.transpose(mem_ref[y, a * 128 : a * 128 + 128, :].astype(F32))
+            memt_ref[:, pl.ds(pl.multiple_of(y * block_rows + a * 128, 128), 128)] = flipped.astype(BF16)
         return c
 
     lax.fori_loop(0, NY, score, 0)
@@ -347,28 +349,36 @@
 
     def last_pass(c):
         await_weights(c)
-        gacc[...] = jnp.zeros_like(gacc)
-
         def block(a, carry):
             start = pl.multiple_of(a * 128, 128)
             at = [pl.ds(start + 8 * v, 8) for v in range(16)]
             acc = weigh(c, at, [ct_ref[at[v], :] for v in range(16)])
-            neg = jnp.transpose(jnp.concatenate(acc, axis=0))
+            neg = jnp.concatenate(acc, axis=0)
+            top = neg.astype(BF16)
+            cneg_ref[pl.ds(start, 128), 0:128] = top
+            cneg_ref[pl.ds(start, 128), 128:256] = (neg - top.astype(F32)).astype(BF16)
             pos = []
             for i in range(NZ):
                 index = inv_ref[i, a]
                 value = lane_gather(wdall[c, i], jnp.bitwise_and(index, 127))
                 pos.append(jnp.where(index >= 0, value, 0.0))
-            cot = neg[:64, :] + neg[64:, :] + jnp.concatenate(pos, axis=0)
-            top = cot.astype(BF16).astype(F32)
-            cot = jnp.concatenate([top, cot - top], axis=0).astype(BF16)
-            memory = mem_ref[lax.div(a, nb), pl.ds(pl.multiple_of(lax.rem(a, nb) * 128, 128), 128), :]
-            gacc[...] = gacc[...] + dot_nn(cot, memory)
+            pos = jnp.concatenate(pos, axis=0)
+            top = pos.astype(BF16)
+            cpos_ref[0:64, pl.ds(start, 128)] = top
+            cpos_ref[64:128, pl.ds(start, 128)] = (pos - top.astype(F32)).astype(BF16)
             return carry
 
-        lax.fori_loop(0, rows // 128, block, 0, unroll=2)
-        grad = gacc[...]
-        gpart[...] = (grad[:64, :] + grad[64:, :]).reshape(NZ, 8, width)
+        lax.fori_loop(0, rows // 128, block, 0, unroll=4)
+        neg = pos = None
+        for y in range(NY):
+            span = slice(y * block_rows, (y + 1) * block_rows)
+            one = dot_nn(memt_ref[:, span], cneg_ref[span, :])
+            two = dot_nn(cpos_ref[:, span], mem_ref[y])
+            neg = one if neg is None else neg + one
+            pos = two if pos is None else pos + two
+        neg = jnp.transpose(neg[:, :128] + neg[:, 128:])
+        grad = neg[:64, :] + neg[64:, :] + pos[:64, :] + pos[64:, :]
+        gpart[...] = grad.reshape(NZ, 8, width)
         to_line(gpart, grs, S_GRAD, GRAD)
         grs[my_z] = gpart[my_z]
 
@@ -379,6 +389,8 @@
     owner_terms(0)
     first_pass(3)
     owner_terms(1)
+    for b in owner:
+        invert_owner(b)
     owner_terms(2)
     second_pass(0)
     owner_terms(3)
@@ -435,7 +447,9 @@
             pltpu.VMEM((NK, own, 128), F32),
             pltpu.VMEM((NK, NZ, own, 128), F32),
             pltpu.VMEM((32, 128), F32),
-            pltpu.VMEM((2 * NZ * own, width), F32),
+            pltpu.VMEM((width, NY * rows), BF16),
+            pltpu.VMEM((NY * rows, 256), BF16),
+            pltpu.VMEM((128, NY * rows), BF16),
             pltpu.VMEM((NZ, own, width), F32),
             pltpu.VMEM((NZ, own, width), F32),
             pltpu.SemaphoreType.DMA((N_SEND,)),

time: 69.1 us -> 65.4 us (0.946)
  Pallas kernels: 65.8 us -> 62.1 us
    pallas_call x1, Pallas kernels: 65.8 us -> 62.1 us  [on_device(): pl.pallas_call(kernel, out_shape=(jax.ShapeDtypeStruct((own,), F32), jax....]
where the time goes in v6:
time: 65.4 us; the launch traced here: 65.2 us
  Pallas kernels  62.1 us (95%)
  local copies, waits for them, and re-layouts  2.47 us (4%)
    pallas_call x1, Pallas kernels, on_device(): pl.pallas_call(kernel, out_shape=(jax.ShapeDtypeStruct((own,), F32), jax....  62.1 us
    unnamed x4, local copies, waits for them, and re-layouts  2.47 us

profile of v6, /device:TPU:2, one launch (start us, length us, event | category | flops | bytes accessed | tf_op | source)
XLA Modules:
  0.0 65.2 jit_solution(9205078591449301595)
XLA Ops:
  0.6 62.1 %shard_map.77 = (f32[8]{0:T(128)}, f32[8,256]{1,0:T(8,128)}) custom-call(s32[8]{0:T(128)} %lab_ref.1, bf16[8,256]{1,0:T(8,128)(2,1)} %q_ref.1, s32[8,64]{1,0:T(8,128)} %id_ref.1, s32[8,64]{1,0:T(8,128)} %mask_ref.1, s32[8,128]{1,0:T(8,128)} %bitcast.1, bf16[1024,256]{1,0:T(8,128)(2,1)} %mem_hbm.1), custom_call_target="tpu_custom_call" | custom-call | tf_op jit(solution)/shard_map/pallas_call | solution.py:417
  62.7 0.0 copy-start
  62.8 0.7 %copy-done = f32[8]{0:T(128)S(1)} copy-done((f32[8]{0:T(128)S(1)}, f32[8]{0:T(128)}, u32[]{:S(2)}) %copy-start) | copy-done | bytes 56
  63.4 0.5 copy.10
  63.9 1.3 %copy.11 = f32[8,256]{1,0:T(8,128)} copy(f32[8,256]{1,0:T(8,128)} %get-tuple-element.5) | data formatting | bytes 16384
Async XLA Ops:
  62.7 0.7 %copy-start = (f32[8]{0:T(128)S(1)}, f32[8]{0:T(128)}, u32[]{:S(2)}) copy-start(f32[8]{0:T(128)} %get-tuple-element.4) | copy-start | bytes 100

commit v7 on v6

--- a/solution.py
+++ b/solution.py
@@ -16,7 +16,7 @@
 MESH = pl.DeviceIdType.MESH
 NY, NZ = 4, 8
 NK, KB = 4, 8
-G = 32
+G = 16
 JC = 16
 PIECES = 4
 EARLY = ()
@@ -254,7 +254,7 @@
                 acc[2 * i + 1] = acc[2 * i + 1] + (float(G) - two)
             return tuple(acc)
 
-        acc = lax.fori_loop(0, rows // (8 * G), step, (zero,) * (2 * KB), unroll=2)
+        acc = lax.fori_loop(0, rows // (8 * G), step, (zero,) * (2 * KB), unroll=4)
         for i in range(KB):
             racc[i] = acc[2 * i]
             racc[KB + i] = acc[2 * i + 1]
@@ -409,12 +409,18 @@
         await_bytes(send_sem, S_WEIGHT, wdall.at[c, pl.ds(0, NZ - 1)])
 
 
+def hand_over(prec_in, grad_in, prec_out, grad_out):
+    for i in range(8):
+        prec_out[i] = prec_in[i]
+    grad_out[...] = grad_in[...]
+
+
 def on_device(queries, query_labels, positive_ids, positive_mask, memory, memory_labels):
     own, width = queries.shape
     rows = memory.shape[0]
     vmem = pl.BlockSpec(memory_space=pltpu.VMEM)
     smem = pl.BlockSpec(memory_space=pltpu.SMEM)
-    return pl.pallas_call(
+    precision, grad = pl.pallas_call(
         kernel,
         out_shape=(
             jax.ShapeDtypeStruct((own,), F32),
@@ -463,6 +469,15 @@
         query_labels, queries, positive_ids, positive_mask,
         memory_labels.reshape(rows // 128, 128), memory,
     )
+    return pl.pallas_call(
+        hand_over,
+        out_shape=(
+            jax.ShapeDtypeStruct((own,), F32),
+            jax.ShapeDtypeStruct((own, width), F32),
+        ),
+        in_specs=[smem, vmem],
+        out_specs=(smem, vmem),
+    )(precision, grad)
 
 
 def solution(mesh):

time: 65.4 us -> 64.1 us (0.980)
  local copies, waits for them, and re-layouts: 2.47 us -> 0 us
  Pallas kernels: 62.1 us -> 63.3 us
    unnamed x4 -> x0, local copies, waits for them, and re-layouts: 2.47 us -> none
    pallas_call x0 -> x1, Pallas kernels: none -> 1.32 us  [on_device(): pl.pallas_call(hand_over, out_shape=(jax.ShapeDtypeStruct((own,), F32), j...]
where the time goes in v7:
time: 64.1 us; the launch traced here: 63.9 us
  Pallas kernels  63.3 us (99%)
    pallas_call x1, Pallas kernels, on_device(): pl.pallas_call(kernel, out_shape=(jax.ShapeDtypeStruct((own,), F32), jax....  62 us
    pallas_call x1, Pallas kernels, on_device(): pl.pallas_call(hand_over, out_shape=(jax.ShapeDtypeStruct((own,), F32), j...  1.32 us

profile of v7, /device:TPU:2, one launch (start us, length us, event | category | flops | bytes accessed | tf_op | source)
XLA Modules:
  0.0 63.9 jit_solution(1289308064865007763)
XLA Ops:
  0.6 62.0 %shard_map.77 = (f32[8]{0:T(128)}, f32[8,256]{1,0:T(8,128)}) custom-call(s32[8]{0:T(128)} %lab_ref.1, bf16[8,256]{1,0:T(8,128)(2,1)} %q_ref.1, s32[8,64]{1,0:T(8,128)} %id_ref.1, s32[8,64]{1,0:T(8,128)} %mask_ref.1, s32[8,128]{1,0:T(8,128)} %bitcast.1, bf16[1024,256]{1,0:T(8,128)(2,1)} %mem_hbm.1), custom_call_target="tpu_custom_call" | custom-call | tf_op jit(solution)/shard_map/pallas_call | solution.py:423
  62.6 1.3 %shard_map.78 = (f32[8]{0:T(128)}, f32[8,256]{1,0:T(8,128)}) custom-call(f32[8]{0:T(128)} %get-tuple-element.4.prec_in, f32[8,256]{1,0:T(8,128)} %get-tuple-element.5.grad_in), custom_call_target="tpu_custom_call" | custom-call | tf_op jit(solution)/shard_map/pallas_call | solution.py:472

commit v8 on v7

--- a/solution.py
+++ b/solution.py
@@ -200,7 +200,7 @@
     on_line(ppart, pz, S_POS, POS)
     pz[my_z] = ppart[...]
 
-    for _ in range(2):
+    for _ in range(3):
         invert_owner(next(owner))
     await_bytes(recv_sem, LAB, labs.at[pl.ds(0, NY - 1)])
     queries = jnp.concatenate([queries, queries], axis=0)

time: 64.1 us -> 63.4 us (0.989)
  Pallas kernels: 63.3 us -> 62.6 us
    pallas_call x1, Pallas kernels: 62 us -> 61.3 us  [on_device(): pl.pallas_call(kernel, out_shape=(jax.ShapeDtypeStruct((own,), F32), jax....]
where the time goes in v8:
time: 63.4 us; the launch traced here: 63.2 us
  Pallas kernels  62.6 us (99%)
  between operations  0.64 us (1%)
    pallas_call x1, Pallas kernels, on_device(): pl.pallas_call(kernel, out_shape=(jax.ShapeDtypeStruct((own,), F32), jax....  61.3 us
    pallas_call x1, Pallas kernels, on_device(): pl.pallas_call(hand_over, out_shape=(jax.ShapeDtypeStruct((own,), F32), j...  1.32 us

profile of v8, /device:TPU:2, one launch (start us, length us, event | category | flops | bytes accessed | tf_op | source)
XLA Modules:
  0.0 63.2 jit_solution(5444761341076497108)
XLA Ops:
  0.6 61.3 %shard_map.77 = (f32[8]{0:T(128)}, f32[8,256]{1,0:T(8,128)}) custom-call(s32[8]{0:T(128)} %lab_ref.1, bf16[8,256]{1,0:T(8,128)(2,1)} %q_ref.1, s32[8,64]{1,0:T(8,128)} %id_ref.1, s32[8,64]{1,0:T(8,128)} %mask_ref.1, s32[8,128]{1,0:T(8,128)} %bitcast.1, bf16[1024,256]{1,0:T(8,128)(2,1)} %mem_hbm.1), custom_call_target="tpu_custom_call" | custom-call | tf_op jit(solution)/shard_map/pallas_call | solution.py:423
  61.9 1.3 %shard_map.78 = (f32[8]{0:T(128)}, f32[8,256]{1,0:T(8,128)}) custom-call(f32[8]{0:T(128)} %get-tuple-element.4.prec_in, f32[8,256]{1,0:T(8,128)} %get-tuple-element.5.grad_in), custom_call_target="tpu_custom_call" | custom-call | tf_op jit(solution)/shard_map/pallas_call | solution.py:472

commit v9 on v8

--- a/solution.py
+++ b/solution.py
@@ -368,7 +368,7 @@
             cpos_ref[64:128, pl.ds(start, 128)] = (pos - top.astype(F32)).astype(BF16)
             return carry
 
-        lax.fori_loop(0, rows // 128, block, 0, unroll=4)
+        lax.fori_loop(0, rows // 128, block, 0, unroll=8)
         neg = pos = None
         for y in range(NY):
             span = slice(y * block_rows, (y + 1) * block_rows)

time: 63.4 us -> 63.3 us (level)
  no operation moved by 1% of the time
where the time goes in v9:
time: 63.3 us; the launch traced here: 63.2 us
  Pallas kernels  62.5 us (99%)
  between operations  0.64 us (1%)
    pallas_call x1, Pallas kernels, on_device(): pl.pallas_call(kernel, out_shape=(jax.ShapeDtypeStruct((own,), F32), jax....  61.2 us
    pallas_call x1, Pallas kernels, on_device(): pl.pallas_call(hand_over, out_shape=(jax.ShapeDtypeStruct((own,), F32), j...  1.32 us

profile of v9, /device:TPU:2, one launch (start us, length us, event | category | flops | bytes accessed | tf_op | source)
XLA Modules:
  0.0 63.2 jit_solution(6096861770013709875)
XLA Ops:
  0.6 61.2 %shard_map.77 = (f32[8]{0:T(128)}, f32[8,256]{1,0:T(8,128)}) custom-call(s32[8]{0:T(128)} %lab_ref.1, bf16[8,256]{1,0:T(8,128)(2,1)} %q_ref.1, s32[8,64]{1,0:T(8,128)} %id_ref.1, s32[8,64]{1,0:T(8,128)} %mask_ref.1, s32[8,128]{1,0:T(8,128)} %bitcast.1, bf16[1024,256]{1,0:T(8,128)(2,1)} %mem_hbm.1), custom_call_target="tpu_custom_call" | custom-call | tf_op jit(solution)/shard_map/pallas_call | solution.py:423
  61.8 1.3 %shard_map.78 = (f32[8]{0:T(128)}, f32[8,256]{1,0:T(8,128)}) custom-call(f32[8]{0:T(128)} %get-tuple-element.4.prec_in, f32[8,256]{1,0:T(8,128)} %get-tuple-element.5.grad_in), custom_call_target="tpu_custom_call" | custom-call | tf_op jit(solution)/shard_map/pallas_call | solution.py:472
